TPU v7x, 512 devices: a whole 4x8x8 slice. The times are simulated.
512 devices in a mesh: exp: 16 (over y, z_hi), skyx: 8 (over z_lo, core), skyy: 4 (over x).
Axes of the slice: x: 4, y: 8, z: 8 (z_hi: 2, z_lo: 4; z = z_hi * 4 + z_lo), core: 2. Of those that a mesh axis runs over, the one named last changes fastest.
Arguments:
- estimate: float32 [2048, 1024], P('skyx', 'skyy'), may hold values from 0.5 to 102
- observed: float32 [16, 2048, 1024], P('exp', 'skyx', 'skyy'), may hold values from 0.25 to 4
- psf_bank: float32 [16, 4, 65, 65], P('exp'), may hold values from 0.1 to 1
- psf_index: int32 [16, 8, 4], P('exp'), may hold values from 0 to 3
- coverage: int32 [16, 8, 4], replicated, may hold values from 0 to 1, as said below
Outputs:
- updated: float32 [2048, 1024], P('skyx', 'skyy')
Inputs may be any that keep to these rules, and one draw needn't show every extreme that they name: `coverage`: every tile is covered by at least one exposure.
All inputs are finite; a program needn't handle non-finite values.
Results may differ from a plain program's by a relative error of at most 0.0003.
Values sent between devices are 32-bit elements; how exact they have to be, the bound alone decides.
No kernel may reach another device: no remote copies, remote signals or barrier semaphores. Data moves between devices by JAX's collectives and lax.ppermute only.
A program may use at most 64 MiB of HBM per device.

v0:
```python
import functools

import jax
import jax.numpy as jnp
import numpy as np
from jax import lax
from jax.experimental import pallas as pl
from jax.experimental.pallas import tpu as pltpu
from jax.sharding import Mesh
from jax.sharding import PartitionSpec as P

TILE = 256
RADIUS = 32
SIDE = 2 * RADIUS + 1
MARGIN = 2 * RADIUS
LANES = 128
FRAME = TILE + 2 * MARGIN
HALF = FRAME // 2
BLOCK = 256
HALO = MARGIN + RADIUS
MODELS = 4
REACH = TILE + 2 * RADIUS
FOLD = REACH // 2
DEPTH = 80
PAIRED = True


def halves(table):
    table = np.asarray(table, np.float32)
    high = table.astype(jnp.bfloat16)
    low = (table - high.astype(np.float32)).astype(jnp.bfloat16)
    return high, low


def waves(places, length):
    frequency = np.arange(length // 2, dtype=np.float64) + 0.5
    angle = 2.0 * np.pi / length * frequency[:, None] * np.asarray(places, np.float64)[None, :]
    return np.concatenate([np.cos(angle), np.sin(angle)], axis=0)


@functools.cache
def tables():
    own = np.arange(MARGIN, HALF) + 0.5
    near = np.arange(RADIUS, MARGIN) + 0.5
    far = np.arange(RADIUS) + 0.5
    margin = np.arange(MARGIN) + 0.5
    starts = (-MARGIN, TILE // 2 - RADIUS)
    column_in = []
    column_out = []
    column_back = []
    for block, start in enumerate(starts):
        column = np.arange(BLOCK) + block * LANES - MARGIN
        place = column - start
        used = (place >= 0) & (place < BLOCK - RADIUS)
        column_in.append((waves(place, BLOCK) * used[None, :]).T)
        first, last = (-RADIUS, LANES) if block == 0 else (LANES, TILE + RADIUS)
        wanted = (column >= first) & (column < last)
        column_out.append(waves(place, BLOCK) * wanted[None, :])
        column_back.append(waves(np.arange(LANES) + block * LANES - start, BLOCK))
    offsets = np.arange(LANES) - RADIUS
    inside = offsets <= RADIUS
    kernel_rows = (waves(offsets, FRAME) * inside[None, :])[:, :DEPTH]
    kernel_cols = (waves(offsets, BLOCK) * inside[None, :]).T

    def across(table):
        high, low = halves(table)
        return np.concatenate([high, high, low], axis=1)

    def pair(table):
        return np.concatenate(halves(table), axis=0)

    def both(places, build=lambda t: t):
        full = waves(places, FRAME)
        return np.concatenate([across(build(full[:HALF])), across(build(full[HALF:]))], axis=0)

    every = np.concatenate([own, near, far])
    ready = np.zeros((FRAME + 3 * BLOCK, BLOCK + 3 * LANES), jnp.bfloat16)
    ready[0:FRAME, 0 : 3 * DEPTH] = across(kernel_rows)
    ready[0:FRAME, BLOCK:] = both(own)
    ready[FRAME : FRAME + 2 * BLOCK, 0 : 2 * BLOCK] = pair(np.concatenate(column_in, axis=1))
    ready[FRAME + 2 * BLOCK :, 0:BLOCK] = pair(kernel_cols)
    return {
        "ready": ready,
        "row_margin": both(margin),
        "row_in": both(every),
        "row_out": both(np.concatenate([own, near]), lambda t: t.T),
        "col_in": pair(np.concatenate(column_in, axis=1)),
        "col_out": pair(np.concatenate(column_out, axis=1)),
        "col_back": pair(np.concatenate(column_back, axis=1)),
    }


def split(value):
    high = value.astype(jnp.bfloat16)
    low = (value - high.astype(jnp.float32)).astype(jnp.bfloat16)
    return high, low


def matmul(left, right):
    return jnp.dot(left, right, preferred_element_type=jnp.float32)


def put_across(ref, rows, value):
    width = value.shape[1]
    ref[rows, 0:width], ref[rows, width : 2 * width] = split(value)


def put_down(ref, row, depth, value, cols=slice(None)):
    count = value.shape[0]
    ref[row : row + count, cols], ref[depth + row : depth + row + count, cols] = split(value)


def across3(ref, rows, first, width, total):
    high = ref[rows, first : first + width]
    return jnp.concatenate([high, ref[rows, total + first : total + first + width], high], axis=1)


def table3(ref, cols=slice(None)):
    depth = ref.shape[0] // 2
    high = ref[0:depth, cols]
    return jnp.concatenate([high, high, ref[depth:, cols]], axis=0)


def data3(ref, first, depth, total, cols=slice(None)):
    high = ref[first : first + depth, cols]
    return jnp.concatenate([high, ref[total + first : total + first + depth, cols], high], axis=0)


def reverse(value):
    count = value.shape[0]
    i = lax.broadcasted_iota(jnp.int32, (count, count), 0)
    j = lax.broadcasted_iota(jnp.int32, (count, count), 1)
    swap = jnp.where(i + j == count - 1, 1.0, 0.0).astype(jnp.bfloat16)
    high, low = split(value)
    return matmul(swap, high) + matmul(swap, low)


def turn(value):
    return pltpu.roll(value, MARGIN, 1)


def low_lanes(rows):
    return lax.broadcasted_iota(jnp.int32, (rows, LANES), 1) < MARGIN


def window_rows(own_ref, left, right, rows):
    low = low_lanes(left.shape[0])
    one, two = turn(own_ref[rows, 0:LANES]), turn(own_ref[rows, LANES:TILE])
    return jnp.concatenate(
        [jnp.where(low, left, one), jnp.where(low, one, two), jnp.where(low, two, right)], axis=1
    )


def fetch(pairs, sems):
    copies = [
        pltpu.make_async_copy(source, target, sems.at[slot])
        for slot, (source, target) in enumerate(pairs)
    ]
    for copy in copies:
        copy.start()
    return copies


def is_even(place_ref):
    return lax.rem(place_ref[0], 2) == 0 if PAIRED else True


def sides_kernel(col_ref, est_ref, obs_ref, even_ref, odd_ref, own_ref, frame_ref, sems):
    for copy in fetch(((est_ref, own_ref), (obs_ref, frame_ref)), sems):
        copy.wait()
    low = low_lanes(TILE)
    first = jnp.where(low, frame_ref[:, 0:LANES], turn(own_ref[:, 0:LANES]))
    last = jnp.where(low, turn(own_ref[:, LANES:TILE]), frame_ref[:, LANES:TILE])
    even = is_even(col_ref)
    even_ref[...] = jnp.where(even, last, first)
    odd_ref[...] = jnp.where(even, first, last)


def ends_kernel(row_ref, col_ref, est_ref, obs_ref, side_even_ref, side_odd_ref, even_ref, odd_ref):
    left, right = ordered(col_ref, side_even_ref, side_odd_ref)
    ends = []
    for est_first, obs_first in ((0, 0), (TILE - MARGIN, TILE - RADIUS)):
        rows = slice(est_first, est_first + MARGIN)
        top = window_rows(est_ref, left(rows), right(rows), rows)
        rows = slice(obs_first, obs_first + RADIUS)
        low = window_rows(obs_ref, turn(left(rows)), turn(right(rows)), rows)
        ends.append((top, low))
    even = is_even(row_ref)
    for part, rows in ((0, slice(0, MARGIN)), (1, slice(MARGIN, HALO))):
        even_ref[rows, :] = jnp.where(even, ends[1][part], ends[0][part])
        odd_ref[rows, :] = jnp.where(even, ends[0][part], ends[1][part])


def ordered(place_ref, even_ref, odd_ref):
    even = is_even(place_ref)
    before = lambda rows: jnp.where(even, odd_ref[rows, :], even_ref[rows, :])
    after = lambda rows: jnp.where(even, even_ref[rows, :], odd_ref[rows, :])
    return before, after


def paired(top, low, near, far):
    a, b, c, d = top[:, near], top[:, far], low[:, near], low[:, far]
    return a - d, b + c, a + d, b - c


def analyse(fold_ref, first, count, col_in_ref, sums_ref):
    for block in range(2):
        cols = slice(block * BLOCK, (block + 1) * BLOCK)
        left = across3(fold_ref, slice(first, first + 2 * count), block * LANES, BLOCK, FRAME)
        put_down(sums_ref, 0, 2 * count, matmul(left, table3(col_in_ref, cols)), cols)


def spectrum(row_ref, sums_ref, count, spec_ref, add):
    for block in range(2):
        near = slice(block * BLOCK, block * BLOCK + LANES)
        far = slice(block * BLOCK + LANES, (block + 1) * BLOCK)
        cols = slice(block * BLOCK, (block + 1) * BLOCK)
        top = matmul(row_ref[0:HALF, :], data3(sums_ref, 0, count, 2 * count, cols))
        low = matmul(row_ref[HALF:FRAME, :], data3(sums_ref, count, count, 2 * count, cols))
        parts = paired(top, low, slice(0, LANES), slice(LANES, BLOCK))
        for part, rows, lanes in zip(
            parts,
            (slice(0, HALF), slice(0, HALF), slice(HALF, FRAME), slice(HALF, FRAME)),
            (near, far, near, far),
            strict=True,
        ):
            spec_ref[rows, lanes] = add[rows, lanes] + part if add is not None else part


def prepare_kernel(
    col_ref, est_ref, obs_ref, side_even_ref, side_odd_ref, bank_ref, table_ref,
    kern_ref, spec_ref, frame_ref,
    raw_ref, wide_ref, tall_ref, fold_ref, sums_ref,
):
    row_own_ref = table_ref.at[0:FRAME, BLOCK : BLOCK + 3 * LANES]
    col_in_ref = table_ref.at[FRAME : FRAME + 2 * BLOCK, 0 : 2 * BLOCK]
    kernel_cols_ref = table_ref.at[FRAME + 2 * BLOCK : FRAME + 3 * BLOCK, 0:BLOCK]
    left, right = ordered(col_ref, side_even_ref, side_odd_ref)
    upper, under = slice(0, LANES), slice(LANES, TILE)
    top = window_rows(est_ref, left(upper), right(upper), upper)
    low = reverse(window_rows(est_ref, left(under), right(under), under))
    put_across(fold_ref, slice(0, LANES), top - low)
    put_across(fold_ref, slice(LANES, TILE), top + low)
    frame_ref[upper, :] = window_rows(obs_ref, turn(left(upper)), turn(right(upper)), upper)
    frame_ref[under, :] = reverse(window_rows(obs_ref, turn(left(under)), turn(right(under)), under))

    shape = (SIDE, SIDE)
    a = lax.broadcasted_iota(jnp.int32, shape, 0).astype(jnp.float32) - RADIUS
    b = lax.broadcasted_iota(jnp.int32, shape, 1).astype(jnp.float32) - RADIUS
    envelope = jnp.exp(-(a * a + b * b) / (2.0 * (0.625 * RADIUS) ** 2))
    raw_ref[...] = jnp.zeros_like(raw_ref)
    for model in range(MODELS):
        raw = bank_ref[:, model, :] * envelope
        total = jnp.sum(jnp.sum(raw, axis=1, keepdims=True), axis=0, keepdims=True)
        raw_ref[model * DEPTH : model * DEPTH + SIDE, 0:SIDE] = raw / total
    put_across(wide_ref, slice(None), raw_ref[...])
    part = matmul(across3(wide_ref, slice(None), 0, LANES, LANES), table3(kernel_cols_ref))
    for model in range(MODELS):
        put_down(tall_ref, 2 * DEPTH * model, DEPTH, part[model * DEPTH : (model + 1) * DEPTH, :])
    gain = 2.0 / (FRAME * BLOCK)
    for model in range(MODELS):
        right = data3(tall_ref, 2 * DEPTH * model, DEPTH, DEPTH)
        top = matmul(table_ref[0:HALF, 0 : 3 * DEPTH], right)
        low = matmul(table_ref[HALF:FRAME, 0 : 3 * DEPTH], right)
        parts = paired(top, low, slice(0, LANES), slice(LANES, BLOCK))
        kern_ref[model, 0:HALF, 0:LANES] = parts[0] * gain
        kern_ref[model, 0:HALF, LANES:BLOCK] = parts[1] * gain
        kern_ref[model, HALF:FRAME, 0:LANES] = parts[2] * gain
        kern_ref[model, HALF:FRAME, LANES:BLOCK] = parts[3] * gain

    analyse(fold_ref, 0, LANES, col_in_ref, sums_ref)
    spectrum(row_own_ref, sums_ref, LANES, spec_ref, None)


def product(spec_ref, kern, block, sign, grown, first, last):
    near = slice(block * BLOCK, block * BLOCK + LANES)
    far = slice(block * BLOCK + LANES, (block + 1) * BLOCK)
    top, low = slice(first, last), slice(HALF + first, HALF + last)
    out = []
    for rows in (top, low):
        fr, fi = spec_ref[rows, near], spec_ref[rows, far]
        kr, ki = kern[rows, 0:LANES], kern[rows, LANES:BLOCK]
        if sign > 0:
            out.append((fr * kr - fi * ki, fr * ki + fi * kr))
        else:
            out.append((fr * kr + fi * ki, fi * kr - fr * ki))
    (ur, ui), (vr, vi) = out
    cos_ref, sin_ref = grown
    put_down(cos_ref, first, HALF, ur + vr, slice(0, LANES))
    put_down(cos_ref, first, HALF, ui + vi, slice(LANES, BLOCK))
    put_down(sin_ref, first, HALF, ui - vi, slice(0, LANES))
    put_down(sin_ref, first, HALF, vr - ur, slice(LANES, BLOCK))


def update_kernel(
    member_ref, row_ref, col_ref, index_ref, cover_ref,
    est_ref, frame_ref, end_even_ref, end_odd_ref, kern_ref, part_ref,
    row_margin_ref, row_in_ref, row_out_ref, col_in_ref, col_out_ref, col_back_ref,
    out_ref,
    fold_ref, sums_ref, spec_ref, cos0_ref, sin0_ref, cos1_ref, sin1_ref, mid0_ref, mid1_ref,
    blur_ref, pick_ref, mask_ref,
):
    member, tile_row, tile_col = member_ref[0], row_ref[0], col_ref[0]
    rows_of_tiles, cols_of_tiles, exposures = cover_ref.shape
    grown = ((cos0_ref, sin0_ref), (cos1_ref, sin1_ref))
    mids = (mid0_ref, mid1_ref)

    above, below = ordered(row_ref, end_even_ref, end_odd_ref)
    top = above(slice(0, MARGIN))
    low = reverse(below(slice(0, MARGIN)))
    put_across(fold_ref, slice(0, MARGIN), top - low)
    put_across(fold_ref, slice(MARGIN, 2 * MARGIN), top + low)
    analyse(fold_ref, 0, MARGIN, col_in_ref, sums_ref)
    spectrum(row_margin_ref, sums_ref, MARGIN, spec_ref, part_ref)

    lane = lax.broadcasted_iota(jnp.int32, (RADIUS, FRAME), 1)
    for step, spans in ((-1, ((LANES, RADIUS),)), (0, ((0, LANES), (FOLD, LANES))), (1, ((FOLD + LANES, RADIUS),))):
        near = []
        for side in (-1, 0, 1):
            r, c = tile_row + step, tile_col + side
            inside = (r >= 0) & (r < rows_of_tiles) & (c >= 0) & (c < cols_of_tiles)
            r = jnp.clip(r, 0, rows_of_tiles - 1)
            c = jnp.clip(c, 0, cols_of_tiles - 1)
            near.append((index_ref[c, r], jnp.where(inside, cover_ref[r, c, member], 0)))

        def spread(which, near=near):
            middle = jnp.where(lane < MARGIN + TILE, near[1][which], near[2][which])
            return jnp.where(lane < MARGIN, near[0][which], middle)

        pick = spread(0)
        cover = jnp.where((lane >= RADIUS) & (lane < FRAME - RADIUS), spread(1), 0)
        for first, count in spans:
            for row in range(first, first + count, RADIUS):
                pick_ref[row : row + RADIUS, :] = pick
                mask_ref[row : row + RADIUS, :] = cover

    def rows_back(block, count, step=None):
        cos_ref, sin_ref = grown[block]
        even = matmul(row_out_ref[0:count, :], data3(cos_ref, 0, HALF, HALF))
        if step is not None:
            step(0)
        odd = matmul(row_out_ref[FOLD : FOLD + count, :], data3(sin_ref, 0, HALF, HALF))
        if step is not None:
            step(1)
        put_across(mids[block], slice(0, count), odd + even)
        put_across(mids[block], slice(count, 2 * count), odd - even)

    def grow(model, block, sign):
        def step(part):
            for first in range(part * HALF // 2, (part + 1) * HALF // 2, 48):
                product(spec_ref, kern_ref.at[model], block, sign, grown[block], first, first + 48)

        return step

    def forward(model, carry):
        rows_back(0, FOLD, grow(model, 1, 1))
        later = jnp.minimum(model + 1, MODELS - 1)
        rows_back(1, FOLD, grow(later, 0, 1))
        one, two = (
            matmul(
                across3(mids[block], slice(0, REACH), 0, BLOCK, BLOCK),
                table3(col_out_ref, slice(block * BLOCK, (block + 1) * BLOCK)),
            )
            for block in range(2)
        )
        for lanes, value in (
            (slice(0, LANES), one[:, 0:LANES]),
            (slice(LANES, BLOCK), one[:, LANES:BLOCK] + two[:, 0:LANES]),
            (slice(BLOCK, FRAME), two[:, LANES:BLOCK]),
        ):
            blur_ref[:, lanes] = jnp.where(pick_ref[:, lanes] == model, value, blur_ref[:, lanes])
        return carry

    grow(0, 0, 1)(0)
    grow(0, 0, 1)(1)
    lax.fori_loop(0, MODELS, forward, 0)

    def ratio(rows, values):
        return jnp.where(mask_ref[rows, :] != 0, values / blur_ref[rows, :], 0.0)

    spare = jnp.zeros((RADIUS, 2 * FRAME), jnp.bfloat16)
    fold_ref[FOLD:HALF, :] = spare
    fold_ref[HALF + FOLD : FRAME, :] = spare
    for row in range(0, LANES, 64):
        top = ratio(slice(row, row + 64), frame_ref[row : row + 64, :])
        low = ratio(slice(FOLD + row, FOLD + row + 64), frame_ref[LANES + row : LANES + row + 64, :])
        put_across(fold_ref, slice(row, row + 64), top - low)
        put_across(fold_ref, slice(HALF + row, HALF + row + 64), top + low)
    top = ratio(slice(LANES, FOLD), above(slice(MARGIN, HALO)))
    low = ratio(slice(FOLD + LANES, REACH), reverse(below(slice(MARGIN, HALO))))
    put_across(fold_ref, slice(LANES, FOLD), top - low)
    put_across(fold_ref, slice(HALF + LANES, HALF + FOLD), top + low)
    analyse(fold_ref, 0, HALF, col_in_ref, sums_ref)
    spectrum(row_in_ref, sums_ref, HALF, spec_ref, None)

    own_model = index_ref[tile_col, tile_row]
    covering = lax.fori_loop(0, exposures, lambda e, n: n + cover_ref[tile_row, tile_col, e], 0)
    own_cover = cover_ref[tile_row, tile_col, member].astype(jnp.float32)
    weight = jnp.full((1, LANES), own_cover, jnp.float32) / jnp.full((1, LANES), covering.astype(jnp.float32), jnp.float32)
    grow(own_model, 0, -1)(0)
    grow(own_model, 0, -1)(1)
    rows_back(0, LANES, grow(own_model, 1, -1))
    rows_back(1, LANES)
    for block in range(2):
        own = slice(block * LANES, (block + 1) * LANES)
        back = matmul(across3(mids[block], slice(0, TILE), 0, BLOCK, BLOCK), table3(col_back_ref, own)) * weight
        out_ref[0:LANES, own] = est_ref[0:LANES, own] * back[0:LANES, :]
        out_ref[LANES:TILE, own] = est_ref[LANES:TILE, own] * reverse(back[LANES:TILE, :])


VMEM = pl.BlockSpec(memory_space=pltpu.VMEM)
SMEM = pl.BlockSpec(memory_space=pltpu.SMEM)


def f32(*shape):
    return jax.ShapeDtypeStruct(shape, jnp.float32)


def half_scratch(*shape):
    return pltpu.VMEM(shape, jnp.bfloat16)


HBM = pl.BlockSpec(memory_space=pltpu.HBM)


def pack_sides(col, estimate, frame):
    return pl.pallas_call(
        sides_kernel,
        out_shape=(f32(TILE, LANES),) * 2 + (f32(TILE, TILE),) * 2,
        in_specs=[SMEM] + [HBM] * 2,
        out_specs=(VMEM,) * 4,
        scratch_shapes=[pltpu.SemaphoreType.DMA((2,))],
        compiler_params=pltpu.CompilerParams(vmem_limit_bytes=4 << 20),
        name="pack_sides",
    )(col, estimate, frame)


def pack_ends(row, col, estimate, frame, side_even, side_odd):
    return pl.pallas_call(
        ends_kernel,
        out_shape=(f32(HALO, FRAME),) * 2,
        in_specs=[SMEM] * 2 + [VMEM] * 4,
        out_specs=(VMEM,) * 2,
        compiler_params=pltpu.CompilerParams(vmem_limit_bytes=4 << 20),
        name="pack_ends",
    )(row, col, estimate, frame, side_even, side_odd)


def prepare(col, estimate, frame, side_even, side_odd, bank, table):
    return pl.pallas_call(
        prepare_kernel,
        out_shape=(f32(MODELS, FRAME, BLOCK), f32(FRAME, 2 * BLOCK), f32(TILE, FRAME)),
        in_specs=[SMEM] + [VMEM] * 6,
        out_specs=(VMEM,) * 3,
        scratch_shapes=[
            pltpu.VMEM((MODELS * DEPTH, LANES), jnp.float32),
            half_scratch(MODELS * DEPTH, 2 * LANES),
            half_scratch(MODELS * 2 * DEPTH, BLOCK),
            half_scratch(TILE, 2 * FRAME),
            half_scratch(2 * TILE, 2 * BLOCK),
        ],
        compiler_params=pltpu.CompilerParams(vmem_limit_bytes=16 << 20),
        cost_estimate=pl.CostEstimate(flops=2 << 30, bytes_accessed=4 << 20, transcendentals=8192),
        name="prepare",
    )(col, estimate, frame, side_even, side_odd, bank, table["ready"])


def tile_update(member, row, col, index, coverage, estimate, frame, end_even, end_odd, spectra, part, table):
    names = ("row_margin", "row_in", "row_out", "col_in", "col_out", "col_back")
    return pl.pallas_call(
        update_kernel,
        out_shape=f32(TILE, TILE),
        in_specs=[SMEM] * 5 + [VMEM] * 12,
        out_specs=VMEM,
        scratch_shapes=[
            half_scratch(FRAME, 2 * FRAME),
            half_scratch(2 * FRAME, 2 * BLOCK),
            pltpu.VMEM((FRAME, 2 * BLOCK), jnp.float32),
            half_scratch(FRAME, BLOCK),
            half_scratch(FRAME, BLOCK),
            half_scratch(FRAME, BLOCK),
            half_scratch(FRAME, BLOCK),
            half_scratch(REACH, 2 * BLOCK),
            half_scratch(REACH, 2 * BLOCK),
            pltpu.VMEM((REACH, FRAME), jnp.float32),
            pltpu.VMEM((REACH, FRAME), jnp.int32),
            pltpu.VMEM((REACH, FRAME), jnp.int32),
        ],
        compiler_params=pltpu.CompilerParams(vmem_limit_bytes=20 << 20),
        cost_estimate=pl.CostEstimate(flops=4 << 30, bytes_accessed=8 << 20, transcendentals=0),
        name="tile_update",
    )(
        member, row, col, index, coverage, estimate, frame, end_even, end_odd, spectra, part,
        *(table[name] for name in names),
    )


def exchange(even, odd, axis):
    count = lax.axis_size(axis)
    if not PAIRED:
        upward = [(i, i + 1) for i in range(count - 1)]
        before = lax.ppermute(even, axis, upward)
        return lax.ppermute(odd, axis, [(b, a) for a, b in upward]), before
    swap = lambda first: [
        step for i in range(first, count - 1, 2) for step in ((i, i + 1), (i + 1, i))
    ]
    outer = lax.ppermute(odd, axis, swap(1))
    return lax.ppermute(even, axis, swap(0)), outer


def exposure_sum(block):
    rows, cols = block.shape
    near = lax.axis_size("exp_y")
    pieces = lax.all_to_all(block.reshape(near, rows // near, cols), "exp_y", 0, 0)
    piece = jnp.sum(pieces, axis=0)
    piece = piece + lax.ppermute(piece, "exp_z", [(0, 1), (1, 0)])
    spread = jnp.broadcast_to(piece[None], (near,) + piece.shape)
    return lax.all_to_all(spread, "exp_y", 0, 0).reshape(rows, cols)


def shards(estimate, observed, psf_bank, psf_index, coverage):
    table = {name: jnp.asarray(value) for name, value in tables().items()}
    frame = observed[0]
    member, row, col = (
        lax.axis_index(axis).astype(jnp.int32).reshape(1)
        for axis in (("exp_y", "exp_z"), "skyx", "skyy")
    )
    bank = psf_bank[0].transpose(1, 0, 2)
    index = psf_index[0].transpose(1, 0)
    cover = coverage.transpose(1, 2, 0)
    *sides, own, frame = pack_sides(col, estimate, frame)
    sides = exchange(*sides, "skyy")
    ends = exchange(*pack_ends(row, col, own, frame, *sides), "skyx")
    spectra, part, folded = prepare(col, own, frame, *sides, bank, table)
    update = tile_update(
        member, row, col, index, cover, own, folded, *ends, spectra, part, table
    )
    return exposure_sum(update)


def solution(mesh):
    exp_count, sky_rows, sky_cols = mesh.devices.shape
    mesh = Mesh(
        mesh.devices.reshape(exp_count // 2, 2, sky_rows, sky_cols),
        ("exp_y", "exp_z", "skyx", "skyy"),
    )
    exp = ("exp_y", "exp_z")
    in_specs = (
        P("skyx", "skyy"),
        P(exp, "skyx", "skyy"),
        P(exp, None, None, None),
        P(exp, None, None),
        P(),
    )
    return jax.shard_map(
        shards, mesh=mesh, in_specs=in_specs, out_specs=P("skyx", "skyy"), check_vma=False
    )
```

profile of v0, /device:TPU:68, one launch (start us, length us, event | category | flops | bytes accessed | tf_op | source)
XLA Modules:
  0.0 75.3 jit_solution(7492187819745766234)
XLA Ops:
  0.0 0.0 copy-start
  0.0 0.9 %copy-done = f32[256,256]{1,0:T(8,128)S(1)} copy-done((f32[256,256]{1,0:T(8,128)S(1)}, f32[256,256]{1,0:T(8,128)}, u32[]{:S(2)}) %copy-start) | copy-done | bytes 262168
  1.0 0.0 copy-start.1
  1.0 0.9 %copy-done.1 = f32[1,256,256]{2,1,0:T(8,128)S(1)} copy-done((f32[1,256,256]{2,1,0:T(8,128)S(1)}, f32[1,256,256]{2,1,0:T(8,128)}, u32[]{:S(2)}) %copy-start.1) | copy-done | bytes 262168
  1.9 0.2 pack_sides.1
  2.1 3.1 %collective-permute-start = (f32[256,128]{1,0:T(8,128)S(1)}, f32[256,128]{1,0:T(8,128)S(1)}, u32[]{:S(2)}, u32[]{:S(2)}) collective-permute-start(f32[256,128]{1,0:T(8,128)S(1)} %get-tuple-element.16), channel_id=1, source_target_pairs={{0,1},{1,0},{2,3},{3,2},{4,5},{5,4},{6,7},{7,6},{8,9},{9,8},{10,11... | collective-permute-start | bytes 393224 | tf_op jit(solution)/shard_map/ppermute | solution.py:508
  5.2 1.9 %collective-permute-start.1 = (f32[256,128]{1,0:T(8,128)S(1)}, f32[256,128]{1,0:T(8,128)S(1)}, u32[]{:S(2)}, u32[]{:S(2)}) collective-permute-start(f32[256,128]{1,0:T(8,128)S(1)} %get-tuple-element.17), channel_id=1, source_target_pairs={{1,2},{2,1},{5,6},{6,5},{9,10},{10,9},{13,14},{14,13},{17,18},{18,... | collective-permute-start | bytes 393224 | tf_op jit(solution)/shard_map/ppermute | solution.py:507
  7.2 2.1 %collective-permute-done.side_even_ref = f32[256,128]{1,0:T(8,128)S(1)} collective-permute-done((f32[256,128]{1,0:T(8,128)S(1)}, f32[256,128]{1,0:T(8,128)S(1)}, u32[]{:S(2)}, u32[]{:S(2)}) %collective-permute-start) | collective-permute-done | bytes 131104 | tf_op jit(solution)/shard_map/ppermute | solution.py:508
  9.2 2.8 %collective-permute-done.1.side_odd_ref = f32[256,128]{1,0:T(8,128)S(1)} collective-permute-done((f32[256,128]{1,0:T(8,128)S(1)}, f32[256,128]{1,0:T(8,128)S(1)}, u32[]{:S(2)}, u32[]{:S(2)}) %collective-permute-start.1) | collective-permute-done | bytes 131104 | tf_op jit(solution)/shard_map/ppermute | solution.py:507
  12.1 0.1 pack_ends.1
  12.2 1.9 %collective-permute-start.2 = (f32[96,384]{1,0:T(8,128)S(1)}, f32[96,384]{1,0:T(8,128)S(1)}, u32[]{:S(2)}, u32[]{:S(2)}) collective-permute-start(f32[96,384]{1,0:T(8,128)S(1)} %get-tuple-element.19), channel_id=1, source_target_pairs={{0,4},{4,0},{8,12},{12,8},{16,20},{20,16},{24,28},{28,24},{1,5},{5... | collective-permute-start | bytes 442376 | tf_op jit(solution)/shard_map/ppermute | solution.py:508
  14.1 4.9 %collective-permute-start.3 = (f32[96,384]{1,0:T(8,128)S(1)}, f32[96,384]{1,0:T(8,128)S(1)}, u32[]{:S(2)}, u32[]{:S(2)}) collective-permute-start(f32[96,384]{1,0:T(8,128)S(1)} %get-tuple-element.20), channel_id=1, source_target_pairs={{4,8},{8,4},{12,16},{16,12},{20,24},{24,20},{5,9},{9,5},{13,17},{1... | collective-permute-start | bytes 442376 | tf_op jit(solution)/shard_map/ppermute | solution.py:507
  19.0 0.0 copy-start.2
  19.0 0.9 %copy-done.2 = f32[1,4,65,65]{3,1,2,0:T(4,128)S(1)} copy-done((f32[1,4,65,65]{3,1,2,0:T(4,128)S(1)}, f32[1,4,65,65]{3,1,2,0:T(4,128)}, u32[]{:S(2)}) %copy-start.2) | copy-done | bytes 67624
  19.9 0.0 copy-start.5
  19.9 1.4 %copy-done.5 = bf16[1152,640]{1,0:T(8,128)(2,1)S(1)} copy-done((bf16[1152,640]{1,0:T(8,128)(2,1)S(1)}, bf16[1152,640]{1,0:T(8,128)(2,1)}, u32[]{:S(2)}) %copy-start.5) | copy-done | bytes 1474584
  21.3 0.0 copy-start.3
  21.3 0.0 copy-start.4
  21.3 0.0 copy-start.6
  21.3 0.0 copy-start.7
  21.3 0.0 copy-start.8
  21.3 0.0 copy-start.9
  21.3 0.0 copy-start.10
  21.4 0.0 copy-start.11
  21.4 1.4 %prepare.1 = (f32[4,384,256]{2,1,0:T(8,128)S(1)}, f32[384,512]{1,0:T(8,128)S(1)}, f32[256,384]{1,0:T(8,128)S(1)}) custom-call(s32[1]{0:T(128)} %bitcast.2.col_ref, f32[256,256]{1,0:T(8,128)S(1)} %get-tuple-element.14.est_ref, f32[256,256]{1,0:T(8,128)S(1)} %get-tuple-element.15.obs_ref, f32[256,128]{1,0:T(8,128)S(1)} %collective-permute-done.side_even_ref, ...), custom_call_target="tpu_custom_call" | custom-call | flops 2147483648 | bytes 4194304 | tf_op jit(solution)/shard_map/prepare/pallas_call | solution.py:450
  22.8 0.0 collective-permute-done.2.end_even_ref
  22.8 0.0 collective-permute-done.3.end_odd_ref
  22.8 0.0 copy-done.3
  22.8 0.0 copy-done.4
  22.8 0.0 copy-done.6
  22.8 0.0 copy-done.7
  22.8 0.0 copy-done.8
  22.8 0.0 copy-done.9
  22.8 0.0 copy-done.10
  22.9 0.1 copy-done.11
  22.9 7.4 %tile_update.1 = f32[256,256]{1,0:T(8,128)S(1)} custom-call(s32[1]{0:T(128)} %bitcast.member_ref, s32[1]{0:T(128)} %bitcast.1.row_ref, s32[1]{0:T(128)} %bitcast.2.col_ref, s32[4,8]{1,0:T(4,128)S(1)} %bitcast.17, s32[8,4,16]{2,1,0:T(4,128)S(1)} %bitcast.16, f32[256,256]{1,0:T(8,128)S(1)} %get-tuple-element.14.est_ref, ...), custom_call_target="tpu_custom_call" | custom-call | flops 4294967296 | bytes 8388608 | tf_op jit(solution)/shard_map/tile_update/pallas_call | solution.py:470
  30.4 17.8 %all_to_all.10 = f32[8,32,256]{2,1,0:T(8,128)S(1)} all-to-all(f32[8,32,256]{2,1,0:T(8,128)S(1)} %bitcast.14), channel_id=1, replica_groups=mesh['exp_y'=8,'exp_z'=2,'skyx'=8,'skyy'=4] {'exp_y'}, dimensions={0} | all-to-all | bytes 524288 | tf_op jit(solution)/shard_map/all_to_all | solution.py:514
  48.1 9.8 %collective-permute-start.4 = (f32[32,256]{1,0:T(8,128)S(1)}, f32[32,256]{1,0:T(8,128)S(1)}, u32[]{:S(2)}, u32[]{:S(2)}) collective-permute-start(f32[32,256]{1,0:T(8,128)S(1)} %reduce_sum.9), channel_id=1, source_target_pairs={{0,32},{32,0},{1,33},{33,1},{2,34},{34,2},{3,35},{35,3},{4,36},{36... | collective-permute-start | bytes 98312 | tf_op jit(solution)/shard_map/ppermute | solution.py:516
  58.0 2.0 %collective-permute-done.4 = f32[32,256]{1,0:T(8,128)S(1)} collective-permute-done((f32[32,256]{1,0:T(8,128)S(1)}, f32[32,256]{1,0:T(8,128)S(1)}, u32[]{:S(2)}, u32[]{:S(2)}) %collective-permute-start.4) | collective-permute-done | bytes 32800 | tf_op jit(solution)/shard_map/ppermute | solution.py:516
  60.0 14.5 %all_to_all.11 = f32[8,32,256]{2,1,0:T(8,128)S(1)} all-to-all(f32[8,32,256]{2,1,0:T(8,128)S(1)} %broadcast_in_dim.2), channel_id=1, replica_groups=mesh['exp_y'=8,'exp_z'=2,'skyx'=8,'skyy'=4] {'exp_y'}, dimensions={0} | all-to-all | bytes 524288 | tf_op jit(solution)/shard_map/all_to_all | solution.py:518
  74.6 0.7 copy.14
  (3 shorter events, 0.0 us)
Async XLA Ops:
  0.0 0.9 %copy-start = (f32[256,256]{1,0:T(8,128)S(1)}, f32[256,256]{1,0:T(8,128)}, u32[]{:S(2)}) copy-start(f32[256,256]{1,0:T(8,128)} %est_ref.1) | copy-start | bytes 786436
  1.0 0.9 %copy-start.1 = (f32[1,256,256]{2,1,0:T(8,128)S(1)}, f32[1,256,256]{2,1,0:T(8,128)}, u32[]{:S(2)}) copy-start(f32[1,256,256]{2,1,0:T(8,128)} %param.13) | copy-start | bytes 786436
  2.1 7.1 %collective-permute-start = (f32[256,128]{1,0:T(8,128)S(1)}, f32[256,128]{1,0:T(8,128)S(1)}, u32[]{:S(2)}, u32[]{:S(2)}) collective-permute-start(f32[256,128]{1,0:T(8,128)S(1)} %get-tuple-element.16), channel_id=1, source_target_pairs={{0,1},{1,0},{2,3},{3,2},{4,5},{5,4},{6,7},{7,6},{8,9},{9,8},{10,11... | collective-permute-start | bytes 393224 | tf_op jit(solution)/shard_map/ppermute | solution.py:508
  5.2 6.9 %collective-permute-start.1 = (f32[256,128]{1,0:T(8,128)S(1)}, f32[256,128]{1,0:T(8,128)S(1)}, u32[]{:S(2)}, u32[]{:S(2)}) collective-permute-start(f32[256,128]{1,0:T(8,128)S(1)} %get-tuple-element.17), channel_id=1, source_target_pairs={{1,2},{2,1},{5,6},{6,5},{9,10},{10,9},{13,14},{14,13},{17,18},{18,... | collective-permute-start | bytes 393224 | tf_op jit(solution)/shard_map/ppermute | solution.py:507
  12.2 10.6 %collective-permute-start.2 = (f32[96,384]{1,0:T(8,128)S(1)}, f32[96,384]{1,0:T(8,128)S(1)}, u32[]{:S(2)}, u32[]{:S(2)}) collective-permute-start(f32[96,384]{1,0:T(8,128)S(1)} %get-tuple-element.19), channel_id=1, source_target_pairs={{0,4},{4,0},{8,12},{12,8},{16,20},{20,16},{24,28},{28,24},{1,5},{5... | collective-permute-start | bytes 442376 | tf_op jit(solution)/shard_map/ppermute | solution.py:508
  14.1 8.6 %collective-permute-start.3 = (f32[96,384]{1,0:T(8,128)S(1)}, f32[96,384]{1,0:T(8,128)S(1)}, u32[]{:S(2)}, u32[]{:S(2)}) collective-permute-start(f32[96,384]{1,0:T(8,128)S(1)} %get-tuple-element.20), channel_id=1, source_target_pairs={{4,8},{8,4},{12,16},{16,12},{20,24},{24,20},{5,9},{9,5},{13,17},{1... | collective-permute-start | bytes 442376 | tf_op jit(solution)/shard_map/ppermute | solution.py:507
  19.0 0.9 %copy-start.2 = (f32[1,4,65,65]{3,1,2,0:T(4,128)S(1)}, f32[1,4,65,65]{3,1,2,0:T(4,128)}, u32[]{:S(2)}) copy-start(f32[1,4,65,65]{3,1,2,0:T(4,128)} %param.14) | copy-start | bytes 202804
  19.9 1.4 %copy-start.5 = (bf16[1152,640]{1,0:T(8,128)(2,1)S(1)}, bf16[1152,640]{1,0:T(8,128)(2,1)}, u32[]{:S(2)}) copy-start(bf16[1152,640]{1,0:T(8,128)(2,1)} %constant.37.clone.table_ref) | copy-start | bytes 4423684
  21.3 1.5 %copy-start.3 = (s32[16,8,4]{0,2,1:T(4,128)S(1)}, s32[16,8,4]{0,2,1:T(4,128)}, u32[]{:S(2)}) copy-start(s32[16,8,4]{0,2,1:T(4,128)} %param.16) | copy-start | bytes 6148
  21.3 1.5 %copy-start.4 = (s32[1,8,4]{1,2,0:T(4,128)S(1)}, s32[1,8,4]{1,2,0:T(4,128)}, u32[]{:S(2)}) copy-start(s32[1,8,4]{1,2,0:T(4,128)} %param.15) | copy-start | bytes 388
  21.3 1.5 %copy-start.6 = (bf16[512,512]{1,0:T(8,128)(2,1)S(1)}, bf16[512,512]{1,0:T(8,128)(2,1)}, u32[]{:S(2)}) copy-start(bf16[512,512]{1,0:T(8,128)(2,1)} %constant.42.clone.col_out_ref) | copy-start | bytes 1572868
  21.3 1.5 %copy-start.7 = (bf16[512,512]{1,0:T(8,128)(2,1)S(1)}, bf16[512,512]{1,0:T(8,128)(2,1)}, u32[]{:S(2)}) copy-start(bf16[512,512]{1,0:T(8,128)(2,1)} %constant.41.clone.col_in_ref) | copy-start | bytes 1572868
  21.3 1.5 %copy-start.8 = (bf16[384,576]{1,0:T(8,128)(2,1)S(1)}, bf16[384,576]{1,0:T(8,128)(2,1)}, u32[]{:S(2)}) copy-start(bf16[384,576]{1,0:T(8,128)(2,1)} %constant.39.clone.row_in_ref) | copy-start | bytes 1327108
  21.3 1.5 %copy-start.9 = (bf16[320,576]{1,0:T(8,128)(2,1)S(1)}, bf16[320,576]{1,0:T(8,128)(2,1)}, u32[]{:S(2)}) copy-start(bf16[320,576]{1,0:T(8,128)(2,1)} %constant.40.clone.row_out_ref) | copy-start | bytes 1105924
  21.3 1.5 %copy-start.10 = (bf16[512,256]{1,0:T(8,128)(2,1)S(1)}, bf16[512,256]{1,0:T(8,128)(2,1)}, u32[]{:S(2)}) copy-start(bf16[512,256]{1,0:T(8,128)(2,1)} %constant.43.clone.col_back_ref) | copy-start | bytes 786436
  21.4 1.6 %copy-start.11 = (bf16[384,192]{1,0:T(8,128)(2,1)S(1)}, bf16[384,192]{1,0:T(8,128)(2,1)}, u32[]{:S(2)}) copy-start(bf16[384,192]{1,0:T(8,128)(2,1)} %constant.38.clone.row_margin_ref) | copy-start | bytes 442372
  48.1 11.8 %collective-permute-start.4 = (f32[32,256]{1,0:T(8,128)S(1)}, f32[32,256]{1,0:T(8,128)S(1)}, u32[]{:S(2)}, u32[]{:S(2)}) collective-permute-start(f32[32,256]{1,0:T(8,128)S(1)} %reduce_sum.9), channel_id=1, source_target_pairs={{0,32},{32,0},{1,33},{33,1},{2,34},{34,2},{3,35},{35,3},{4,36},{36... | collective-permute-start | bytes 98312 | tf_op jit(solution)/shard_map/ppermute | solution.py:516
where the time goes:
time: 75.7 us; the launch traced here: 75.3 us
  blocking collectives  32.3 us (43%)
  starting transfers between devices  21.6 us (29%)
  Pallas kernels  9.14 us (12%)
  waiting for transfers between devices  6.94 us (9%)
  local copies, waits for them, and re-layouts  5.01 us (7%)
    all_to_all x1, blocking collectives, exposure_sum(): lax.all_to_all(block.reshape(near, rows // near, cols), 'exp_y', 0, 0)  17.8 us
    all_to_all x1, blocking collectives, exposure_sum(): return lax.all_to_all(spread, 'exp_y', 0, 0).reshape(rows, cols)  14.5 us
    ppermute x1, starting transfers between devices, exposure_sum(): piece = piece + lax.ppermute(piece, 'exp_z', [(0, 1), (1, 0)])  9.83 us
    pallas_call x1, Pallas kernels, tile_update(): pl.pallas_call(update_kernel, out_shape=f32(TILE, TILE), in_specs=[SMEM]...  7.43 us
    ppermute x2, starting transfers between devices, exchange(): outer = lax.ppermute(odd, axis, swap(1))  6.79 us
    ppermute x2, starting transfers between devices, exchange(): return (lax.ppermute(even, axis, swap(0)), outer)  5.03 us
    unnamed x25, local copies, waits for them, and re-layouts  4.99 us
    ppermute x2, waiting for transfers between devices, exchange(): outer = lax.ppermute(odd, axis, swap(1))  2.85 us
  transfers between devices with their start and end apart: 5, of which 3 were waited for; matrix products, arithmetic and copies ran while one was open for 0% of the time, Pallas kernels for 2%

commit v1 on v0

--- a/solution.py
+++ b/solution.py
@@ -22,7 +22,6 @@
 REACH = TILE + 2 * RADIUS
 FOLD = REACH // 2
 DEPTH = 80
-PAIRED = True
 
 
 def halves(table):
@@ -84,7 +83,6 @@
         "row_margin": both(margin),
         "row_in": both(every),
         "row_out": both(np.concatenate([own, near]), lambda t: t.T),
-        "col_in": pair(np.concatenate(column_in, axis=1)),
         "col_out": pair(np.concatenate(column_out, axis=1)),
         "col_back": pair(np.concatenate(column_back, axis=1)),
     }
@@ -151,33 +149,12 @@
     )
 
 
-def fetch(pairs, sems):
-    copies = [
-        pltpu.make_async_copy(source, target, sems.at[slot])
-        for slot, (source, target) in enumerate(pairs)
-    ]
-    for copy in copies:
-        copy.start()
-    return copies
-
-
 def is_even(place_ref):
-    return lax.rem(place_ref[0], 2) == 0 if PAIRED else True
-
-
-def sides_kernel(col_ref, est_ref, obs_ref, even_ref, odd_ref, own_ref, frame_ref, sems):
-    for copy in fetch(((est_ref, own_ref), (obs_ref, frame_ref)), sems):
-        copy.wait()
-    low = low_lanes(TILE)
-    first = jnp.where(low, frame_ref[:, 0:LANES], turn(own_ref[:, 0:LANES]))
-    last = jnp.where(low, turn(own_ref[:, LANES:TILE]), frame_ref[:, LANES:TILE])
-    even = is_even(col_ref)
-    even_ref[...] = jnp.where(even, last, first)
-    odd_ref[...] = jnp.where(even, first, last)
-
-
-def ends_kernel(row_ref, col_ref, est_ref, obs_ref, side_even_ref, side_odd_ref, even_ref, odd_ref):
-    left, right = ordered(col_ref, side_even_ref, side_odd_ref)
+    return lax.rem(place_ref[0], 2) == 0
+
+
+def ends_kernel(row_ref, est_ref, obs_ref, right_ref, left_ref, even_ref, odd_ref):
+    left, right = (lambda rows: left_ref[rows, :]), (lambda rows: right_ref[rows, :])
     ends = []
     for est_first, obs_first in ((0, 0), (TILE - MARGIN, TILE - RADIUS)):
         rows = slice(est_first, est_first + MARGIN)
@@ -228,14 +205,14 @@
 
 
 def prepare_kernel(
-    col_ref, est_ref, obs_ref, side_even_ref, side_odd_ref, bank_ref, table_ref,
+    est_ref, obs_ref, right_ref, left_ref, bank_ref, table_ref,
     kern_ref, spec_ref, frame_ref,
     raw_ref, wide_ref, tall_ref, fold_ref, sums_ref,
 ):
     row_own_ref = table_ref.at[0:FRAME, BLOCK : BLOCK + 3 * LANES]
     col_in_ref = table_ref.at[FRAME : FRAME + 2 * BLOCK, 0 : 2 * BLOCK]
     kernel_cols_ref = table_ref.at[FRAME + 2 * BLOCK : FRAME + 3 * BLOCK, 0:BLOCK]
-    left, right = ordered(col_ref, side_even_ref, side_odd_ref)
+    left, right = (lambda rows: left_ref[rows, :]), (lambda rows: right_ref[rows, :])
     upper, under = slice(0, LANES), slice(LANES, TILE)
     top = window_rows(est_ref, left(upper), right(upper), upper)
     low = reverse(window_rows(est_ref, left(under), right(under), under))
@@ -295,13 +272,14 @@
 def update_kernel(
     member_ref, row_ref, col_ref, index_ref, cover_ref,
     est_ref, frame_ref, end_even_ref, end_odd_ref, kern_ref, part_ref,
-    row_margin_ref, row_in_ref, row_out_ref, col_in_ref, col_out_ref, col_back_ref,
+    row_margin_ref, row_in_ref, row_out_ref, ready_ref, col_out_ref, col_back_ref,
     out_ref,
     fold_ref, sums_ref, spec_ref, cos0_ref, sin0_ref, cos1_ref, sin1_ref, mid0_ref, mid1_ref,
     blur_ref, pick_ref, mask_ref,
 ):
     member, tile_row, tile_col = member_ref[0], row_ref[0], col_ref[0]
     rows_of_tiles, cols_of_tiles, exposures = cover_ref.shape
+    col_in_ref = ready_ref.at[FRAME : FRAME + 2 * BLOCK, 0 : 2 * BLOCK]
     grown = ((cos0_ref, sin0_ref), (cos1_ref, sin1_ref))
     mids = (mid0_ref, mid1_ref)
 
@@ -420,37 +398,22 @@
     return pltpu.VMEM(shape, jnp.bfloat16)
 
 
-HBM = pl.BlockSpec(memory_space=pltpu.HBM)
-
-
-def pack_sides(col, estimate, frame):
-    return pl.pallas_call(
-        sides_kernel,
-        out_shape=(f32(TILE, LANES),) * 2 + (f32(TILE, TILE),) * 2,
-        in_specs=[SMEM] + [HBM] * 2,
-        out_specs=(VMEM,) * 4,
-        scratch_shapes=[pltpu.SemaphoreType.DMA((2,))],
-        compiler_params=pltpu.CompilerParams(vmem_limit_bytes=4 << 20),
-        name="pack_sides",
-    )(col, estimate, frame)
-
-
-def pack_ends(row, col, estimate, frame, side_even, side_odd):
+def pack_ends(row, estimate, frame, side_even, side_odd):
     return pl.pallas_call(
         ends_kernel,
         out_shape=(f32(HALO, FRAME),) * 2,
-        in_specs=[SMEM] * 2 + [VMEM] * 4,
+        in_specs=[SMEM] + [VMEM] * 4,
         out_specs=(VMEM,) * 2,
         compiler_params=pltpu.CompilerParams(vmem_limit_bytes=4 << 20),
         name="pack_ends",
-    )(row, col, estimate, frame, side_even, side_odd)
-
-
-def prepare(col, estimate, frame, side_even, side_odd, bank, table):
+    )(row, estimate, frame, side_even, side_odd)
+
+
+def prepare(estimate, frame, side_even, side_odd, bank, table):
     return pl.pallas_call(
         prepare_kernel,
         out_shape=(f32(MODELS, FRAME, BLOCK), f32(FRAME, 2 * BLOCK), f32(TILE, FRAME)),
-        in_specs=[SMEM] + [VMEM] * 6,
+        in_specs=[VMEM] * 6,
         out_specs=(VMEM,) * 3,
         scratch_shapes=[
             pltpu.VMEM((MODELS * DEPTH, LANES), jnp.float32),
@@ -462,11 +425,11 @@
         compiler_params=pltpu.CompilerParams(vmem_limit_bytes=16 << 20),
         cost_estimate=pl.CostEstimate(flops=2 << 30, bytes_accessed=4 << 20, transcendentals=8192),
         name="prepare",
-    )(col, estimate, frame, side_even, side_odd, bank, table["ready"])
+    )(estimate, frame, side_even, side_odd, bank, table["ready"])
 
 
 def tile_update(member, row, col, index, coverage, estimate, frame, end_even, end_odd, spectra, part, table):
-    names = ("row_margin", "row_in", "row_out", "col_in", "col_out", "col_back")
+    names = ("row_margin", "row_in", "row_out", "ready", "col_out", "col_back")
     return pl.pallas_call(
         update_kernel,
         out_shape=f32(TILE, TILE),
@@ -497,15 +460,11 @@
 
 def exchange(even, odd, axis):
     count = lax.axis_size(axis)
-    if not PAIRED:
-        upward = [(i, i + 1) for i in range(count - 1)]
-        before = lax.ppermute(even, axis, upward)
-        return lax.ppermute(odd, axis, [(b, a) for a, b in upward]), before
     swap = lambda first: [
         step for i in range(first, count - 1, 2) for step in ((i, i + 1), (i + 1, i))
     ]
-    outer = lax.ppermute(odd, axis, swap(1))
-    return lax.ppermute(even, axis, swap(0)), outer
+    near = lax.ppermute(even, axis, swap(0))
+    return near, lax.ppermute(odd, axis, swap(1))
 
 
 def exposure_sum(block):
@@ -528,10 +487,16 @@
     bank = psf_bank[0].transpose(1, 0, 2)
     index = psf_index[0].transpose(1, 0)
     cover = coverage.transpose(1, 2, 0)
-    *sides, own, frame = pack_sides(col, estimate, frame)
-    sides = exchange(*sides, "skyy")
-    ends = exchange(*pack_ends(row, col, own, frame, *sides), "skyx")
-    spectra, part, folded = prepare(col, own, frame, *sides, bank, table)
+    own = estimate
+    first = jnp.concatenate([frame[:, :MARGIN], own[:, :MARGIN]], axis=1)
+    last = jnp.concatenate([own[:, TILE - MARGIN :], frame[:, TILE - MARGIN :]], axis=1)
+    upward = [(i, i + 1) for i in range(lax.axis_size("skyy") - 1)]
+    sides = (
+        lax.ppermute(first, "skyy", [(b, a) for a, b in upward]),
+        lax.ppermute(last, "skyy", upward),
+    )
+    ends = exchange(*pack_ends(row, own, frame, *sides), "skyx")
+    spectra, part, folded = prepare(own, frame, *sides, bank, table)
     update = tile_update(
         member, row, col, index, cover, own, folded, *ends, spectra, part, table
     )

time: 75.7 us -> 74.4 us (0.983)
  the two profiles are of different devices: /device:TPU:68 before, /device:TPU:64 now
where the time goes in v1:
time: 74.4 us; the launch traced here: 74.1 us
  blocking collectives  32.2 us (43%)
  starting transfers between devices  21.3 us (29%)
  Pallas kernels  9.09 us (12%)
  waiting for transfers between devices  8.88 us (12%)
  local copies, waits for them, and re-layouts  2.16 us (3%)
    all_to_all x1, blocking collectives, exposure_sum(): lax.all_to_all(block.reshape(near, rows // near, cols), 'exp_y', 0, 0)  18.4 us
    all_to_all x1, blocking collectives, exposure_sum(): return lax.all_to_all(spread, 'exp_y', 0, 0).reshape(rows, cols)  13.8 us
    ppermute x1, starting transfers between devices, exposure_sum(): piece = piece + lax.ppermute(piece, 'exp_z', [(0, 1), (1, 0)])  9.77 us
    pallas_call x1, Pallas kernels, tile_update(): pl.pallas_call(update_kernel, out_shape=f32(TILE, TILE), in_specs=[SMEM]...  7.59 us
    ppermute x1, starting transfers between devices, exchange(): return (near, lax.ppermute(odd, axis, swap(1)))  4.89 us
    ppermute x1, waiting for transfers between devices, shards(): lax.ppermute(first, 'skyy', [(b, a) for a, b in upward])  4.24 us
    ppermute x1, starting transfers between devices, shards(): lax.ppermute(last, 'skyy', upward)  3.4 us
    ppermute x1, waiting for transfers between devices, exposure_sum(): piece = piece + lax.ppermute(piece, 'exp_z', [(0, 1), (1, 0)])  2 us
  transfers between devices with their start and end apart: 5, of which 4 were waited for; matrix products, arithmetic and copies ran while one was open for 0% of the time, Pallas kernels for 2%

profile of v1, /device:TPU:64, one launch (start us, length us, event | category | flops | bytes accessed | tf_op | source)
XLA Modules:
  0.0 74.1 jit_solution(5283708404423975828)
XLA Ops:
  0.0 0.0 copy-start
  0.0 0.0 copy-start.1
  0.0 0.0 copy-start.5
  0.0 0.0 copy-start.2
  0.0 1.4 %fusion = (f32[256,64]{1,0:T(8,128)S(1)}, f32[256,64]{1,0:T(8,128)S(1)}, f32[256,64]{1,0:T(8,128)S(1)}, f32[256,64]{1,0:T(8,128)S(1)}) fusion(f32[256,256]{1,0:T(8,128)} %est_ref.5, f32[256,256]{1,0:T(8,128)} %bitcast.13), kind=kLoop, calls=%fused_computation.2 | loop fusion | bytes 524288 | tf_op jit(solution)/shard_map/slice | solution.py:492
  1.4 0.1 pad_maximum_fusion.1
  1.5 3.4 %collective-permute-start.1 = (f32[256,128]{1,0:T(8,128)S(1)}, f32[256,128]{1,0:T(8,128)S(1)}, u32[]{:S(2)}, u32[]{:S(2)}) collective-permute-start(f32[256,128]{1,0:T(8,128)S(1)} %pad_maximum_fusion.1), channel_id=1, source_target_pairs={{0,1},{1,2},{2,3},{4,5},{5,6},{6,7},{8,9},{9,10},{10,11},{12,13},{... | collective-permute-start | bytes 393224 | tf_op jit(solution)/shard_map/ppermute | solution.py:496
  4.9 0.1 pad_maximum_fusion
  5.0 1.3 %collective-permute-start = (f32[256,128]{1,0:T(8,128)S(1)}, f32[256,128]{1,0:T(8,128)S(1)}, u32[]{:S(2)}, u32[]{:S(2)}) collective-permute-start(f32[256,128]{1,0:T(8,128)S(1)} %pad_maximum_fusion), channel_id=1, source_target_pairs={{1,0},{2,1},{3,2},{5,4},{6,5},{7,6},{9,8},{10,9},{11,10},{13,12},{... | collective-permute-start | bytes 393224 | tf_op jit(solution)/shard_map/ppermute | solution.py:495
  6.3 1.3 %collective-permute-done.1.left_ref = f32[256,128]{1,0:T(8,128)S(1)} collective-permute-done((f32[256,128]{1,0:T(8,128)S(1)}, f32[256,128]{1,0:T(8,128)S(1)}, u32[]{:S(2)}, u32[]{:S(2)}) %collective-permute-start.1) | collective-permute-done | bytes 131104 | tf_op jit(solution)/shard_map/ppermute | solution.py:496
  7.6 4.2 %collective-permute-done.right_ref = f32[256,128]{1,0:T(8,128)S(1)} collective-permute-done((f32[256,128]{1,0:T(8,128)S(1)}, f32[256,128]{1,0:T(8,128)S(1)}, u32[]{:S(2)}, u32[]{:S(2)}) %collective-permute-start) | collective-permute-done | bytes 131104 | tf_op jit(solution)/shard_map/ppermute | solution.py:495
  11.9 0.0 copy-done
  11.9 0.0 copy-done.1
  11.9 0.1 pack_ends.1
  12.0 1.9 %collective-permute-start.2 = (f32[96,384]{1,0:T(8,128)S(1)}, f32[96,384]{1,0:T(8,128)S(1)}, u32[]{:S(2)}, u32[]{:S(2)}) collective-permute-start(f32[96,384]{1,0:T(8,128)S(1)} %get-tuple-element.11), channel_id=1, source_target_pairs={{0,4},{4,0},{8,12},{12,8},{16,20},{20,16},{24,28},{28,24},{1,5},{5... | collective-permute-start | bytes 442376 | tf_op jit(solution)/shard_map/ppermute | solution.py:466
  14.0 4.9 %collective-permute-start.3 = (f32[96,384]{1,0:T(8,128)S(1)}, f32[96,384]{1,0:T(8,128)S(1)}, u32[]{:S(2)}, u32[]{:S(2)}) collective-permute-start(f32[96,384]{1,0:T(8,128)S(1)} %get-tuple-element.12), channel_id=1, source_target_pairs={{4,8},{8,4},{12,16},{16,12},{20,24},{24,20},{5,9},{9,5},{13,17},{1... | collective-permute-start | bytes 442376 | tf_op jit(solution)/shard_map/ppermute | solution.py:467
  18.9 0.0 copy-done.5
  18.9 0.0 copy-done.2
  18.9 0.0 copy-start.3
  18.9 0.0 copy-start.4
  18.9 0.0 copy-start.6
  18.9 0.0 copy-start.7
  18.9 0.0 copy-start.8
  18.9 0.0 copy-start.9
  19.0 0.0 copy-start.10
  19.0 1.4 %prepare.1 = (f32[4,384,256]{2,1,0:T(8,128)S(1)}, f32[384,512]{1,0:T(8,128)S(1)}, f32[256,384]{1,0:T(8,128)S(1)}) custom-call(f32[256,256]{1,0:T(8,128)S(1)} %copy-done.1, f32[256,256]{1,0:T(8,128)S(1)} %bitcast.15, f32[256,128]{1,0:T(8,128)S(1)} %collective-permute-done.right_ref, f32[256,128]{1,0:T(8,128)S(1)} %collective-permute-done.1.left_ref, ...), custom_call_target="tpu_custom_call" | custom-call | flops 2147483648 | bytes 4194304 | tf_op jit(solution)/shard_map/prepare/pallas_call | solution.py:413
  20.3 0.0 collective-permute-done.2.end_even_ref
  20.4 1.3 %collective-permute-done.3.end_odd_ref = f32[96,384]{1,0:T(8,128)S(1)} collective-permute-done((f32[96,384]{1,0:T(8,128)S(1)}, f32[96,384]{1,0:T(8,128)S(1)}, u32[]{:S(2)}, u32[]{:S(2)}) %collective-permute-start.3) | collective-permute-done | bytes 147488 | tf_op jit(solution)/shard_map/ppermute | solution.py:467
  21.7 0.0 copy-done.3
  21.7 0.0 copy-done.4
  21.7 0.0 copy-done.6
  21.7 0.0 copy-done.7
  21.7 0.0 copy-done.8
  21.7 0.0 copy-done.9
  21.7 0.0 copy-done.10
  21.7 7.6 %tile_update.1 = f32[256,256]{1,0:T(8,128)S(1)} custom-call(s32[1]{0:T(128)} %bitcast.member_ref, s32[1]{0:T(128)} %bitcast.1.row_ref, s32[1]{0:T(128)} %bitcast.2.col_ref, s32[4,8]{1,0:T(4,128)S(1)} %bitcast.19, s32[8,4,16]{2,1,0:T(4,128)S(1)} %bitcast.18, f32[256,256]{1,0:T(8,128)S(1)} %copy-done.1, f32[256,384]{1,0:T(8,128)S(1)} %get-tuple-element.10.frame_ref, ...), custom_call_target="tpu_custom_call" | custom-call | flops 4294967296 | bytes 8388608 | tf_op jit(solution)/shard_map/tile_update/pallas_call | solution.py:433
  29.3 18.4 %all_to_all.10 = f32[8,32,256]{2,1,0:T(8,128)S(1)} all-to-all(f32[8,32,256]{2,1,0:T(8,128)S(1)} %bitcast.16), channel_id=1, replica_groups=mesh['exp_y'=8,'exp_z'=2,'skyx'=8,'skyy'=4] {'exp_y'}, dimensions={0} | all-to-all | bytes 524288 | tf_op jit(solution)/shard_map/all_to_all | solution.py:473
  47.8 9.8 %collective-permute-start.4 = (f32[32,256]{1,0:T(8,128)S(1)}, f32[32,256]{1,0:T(8,128)S(1)}, u32[]{:S(2)}, u32[]{:S(2)}) collective-permute-start(f32[32,256]{1,0:T(8,128)S(1)} %reduce_sum.9), channel_id=1, source_target_pairs={{0,32},{32,0},{1,33},{33,1},{2,34},{34,2},{3,35},{35,3},{4,36},{36... | collective-permute-start | bytes 98312 | tf_op jit(solution)/shard_map/ppermute | solution.py:475
  57.6 2.0 %collective-permute-done.4 = f32[32,256]{1,0:T(8,128)S(1)} collective-permute-done((f32[32,256]{1,0:T(8,128)S(1)}, f32[32,256]{1,0:T(8,128)S(1)}, u32[]{:S(2)}, u32[]{:S(2)}) %collective-permute-start.4) | collective-permute-done | bytes 32800 | tf_op jit(solution)/shard_map/ppermute | solution.py:475
  59.6 13.8 %all_to_all.11 = f32[8,32,256]{2,1,0:T(8,128)S(1)} all-to-all(f32[8,32,256]{2,1,0:T(8,128)S(1)} %broadcast_in_dim.2), channel_id=1, replica_groups=mesh['exp_y'=8,'exp_z'=2,'skyx'=8,'skyy'=4] {'exp_y'}, dimensions={0} | all-to-all | bytes 524288 | tf_op jit(solution)/shard_map/all_to_all | solution.py:477
  73.4 0.7 copy.13
  (3 shorter events, 0.0 us)
Async XLA Ops:
  0.0 11.9 %copy-start = (f32[1,256,256]{2,1,0:T(8,128)S(1)}, f32[1,256,256]{2,1,0:T(8,128)}, u32[]{:S(2)}) copy-start(f32[1,256,256]{2,1,0:T(8,128)} %param.12) | copy-start | bytes 786436
  0.0 11.9 %copy-start.1 = (f32[256,256]{1,0:T(8,128)S(1)}, f32[256,256]{1,0:T(8,128)}, u32[]{:S(2)}) copy-start(f32[256,256]{1,0:T(8,128)} %est_ref.5) | copy-start | bytes 786436
  0.0 18.9 %copy-start.5 = (bf16[1152,640]{1,0:T(8,128)(2,1)S(1)}, bf16[1152,640]{1,0:T(8,128)(2,1)}, u32[]{:S(2)}) copy-start(bf16[1152,640]{1,0:T(8,128)(2,1)} %constant.35.clone.table_ref.ready_ref) | copy-start | bytes 4423684
  0.0 18.9 %copy-start.2 = (f32[1,4,65,65]{3,1,2,0:T(4,128)S(1)}, f32[1,4,65,65]{3,1,2,0:T(4,128)}, u32[]{:S(2)}) copy-start(f32[1,4,65,65]{3,1,2,0:T(4,128)} %param.13) | copy-start | bytes 202804
  1.5 6.1 %collective-permute-start.1 = (f32[256,128]{1,0:T(8,128)S(1)}, f32[256,128]{1,0:T(8,128)S(1)}, u32[]{:S(2)}, u32[]{:S(2)}) collective-permute-start(f32[256,128]{1,0:T(8,128)S(1)} %pad_maximum_fusion.1), channel_id=1, source_target_pairs={{0,1},{1,2},{2,3},{4,5},{5,6},{6,7},{8,9},{9,10},{10,11},{12,13},{... | collective-permute-start | bytes 393224 | tf_op jit(solution)/shard_map/ppermute | solution.py:496
  5.0 6.9 %collective-permute-start = (f32[256,128]{1,0:T(8,128)S(1)}, f32[256,128]{1,0:T(8,128)S(1)}, u32[]{:S(2)}, u32[]{:S(2)}) collective-permute-start(f32[256,128]{1,0:T(8,128)S(1)} %pad_maximum_fusion), channel_id=1, source_target_pairs={{1,0},{2,1},{3,2},{5,4},{6,5},{7,6},{9,8},{10,9},{11,10},{13,12},{... | collective-permute-start | bytes 393224 | tf_op jit(solution)/shard_map/ppermute | solution.py:495
  12.0 8.3 %collective-permute-start.2 = (f32[96,384]{1,0:T(8,128)S(1)}, f32[96,384]{1,0:T(8,128)S(1)}, u32[]{:S(2)}, u32[]{:S(2)}) collective-permute-start(f32[96,384]{1,0:T(8,128)S(1)} %get-tuple-element.11), channel_id=1, source_target_pairs={{0,4},{4,0},{8,12},{12,8},{16,20},{20,16},{24,28},{28,24},{1,5},{5... | collective-permute-start | bytes 442376 | tf_op jit(solution)/shard_map/ppermute | solution.py:466
  14.0 7.7 %collective-permute-start.3 = (f32[96,384]{1,0:T(8,128)S(1)}, f32[96,384]{1,0:T(8,128)S(1)}, u32[]{:S(2)}, u32[]{:S(2)}) collective-permute-start(f32[96,384]{1,0:T(8,128)S(1)} %get-tuple-element.12), channel_id=1, source_target_pairs={{4,8},{8,4},{12,16},{16,12},{20,24},{24,20},{5,9},{9,5},{13,17},{1... | collective-permute-start | bytes 442376 | tf_op jit(solution)/shard_map/ppermute | solution.py:467
  18.9 2.8 %copy-start.3 = (s32[16,8,4]{0,2,1:T(4,128)S(1)}, s32[16,8,4]{0,2,1:T(4,128)}, u32[]{:S(2)}) copy-start(s32[16,8,4]{0,2,1:T(4,128)} %param.15) | copy-start | bytes 6148
  18.9 2.8 %copy-start.4 = (s32[1,8,4]{1,2,0:T(4,128)S(1)}, s32[1,8,4]{1,2,0:T(4,128)}, u32[]{:S(2)}) copy-start(s32[1,8,4]{1,2,0:T(4,128)} %param.14) | copy-start | bytes 388
  18.9 2.8 %copy-start.6 = (bf16[512,512]{1,0:T(8,128)(2,1)S(1)}, bf16[512,512]{1,0:T(8,128)(2,1)}, u32[]{:S(2)}) copy-start(bf16[512,512]{1,0:T(8,128)(2,1)} %constant.39.clone.col_out_ref) | copy-start | bytes 1572868
  18.9 2.8 %copy-start.7 = (bf16[384,576]{1,0:T(8,128)(2,1)S(1)}, bf16[384,576]{1,0:T(8,128)(2,1)}, u32[]{:S(2)}) copy-start(bf16[384,576]{1,0:T(8,128)(2,1)} %constant.37.clone.row_in_ref) | copy-start | bytes 1327108
  18.9 2.8 %copy-start.8 = (bf16[320,576]{1,0:T(8,128)(2,1)S(1)}, bf16[320,576]{1,0:T(8,128)(2,1)}, u32[]{:S(2)}) copy-start(bf16[320,576]{1,0:T(8,128)(2,1)} %constant.38.clone.row_out_ref) | copy-start | bytes 1105924
  18.9 2.8 %copy-start.9 = (bf16[512,256]{1,0:T(8,128)(2,1)S(1)}, bf16[512,256]{1,0:T(8,128)(2,1)}, u32[]{:S(2)}) copy-start(bf16[512,256]{1,0:T(8,128)(2,1)} %constant.40.clone.col_back_ref) | copy-start | bytes 786436
  19.0 2.8 %copy-start.10 = (bf16[384,192]{1,0:T(8,128)(2,1)S(1)}, bf16[384,192]{1,0:T(8,128)(2,1)}, u32[]{:S(2)}) copy-start(bf16[384,192]{1,0:T(8,128)(2,1)} %constant.36.clone.row_margin_ref) | copy-start | bytes 442372
  47.8 11.8 %collective-permute-start.4 = (f32[32,256]{1,0:T(8,128)S(1)}, f32[32,256]{1,0:T(8,128)S(1)}, u32[]{:S(2)}, u32[]{:S(2)}) collective-permute-start(f32[32,256]{1,0:T(8,128)S(1)} %reduce_sum.9), channel_id=1, source_target_pairs={{0,32},{32,0},{1,33},{33,1},{2,34},{34,2},{3,35},{35,3},{4,36},{36... | collective-permute-start | bytes 98312 | tf_op jit(solution)/shard_map/ppermute | solution.py:475

commit v2 on v1

--- a/solution.py
+++ b/solution.py
@@ -149,30 +149,18 @@
     )
 
 
-def is_even(place_ref):
-    return lax.rem(place_ref[0], 2) == 0
-
-
-def ends_kernel(row_ref, est_ref, obs_ref, right_ref, left_ref, even_ref, odd_ref):
-    left, right = (lambda rows: left_ref[rows, :]), (lambda rows: right_ref[rows, :])
+def ends_kernel(row_ref, est_ref, obs_ref, left_ref, right_ref, pair_ref, outer_ref):
+    even = lax.rem(row_ref[0], 2) == 0
     ends = []
     for est_first, obs_first in ((0, 0), (TILE - MARGIN, TILE - RADIUS)):
         rows = slice(est_first, est_first + MARGIN)
-        top = window_rows(est_ref, left(rows), right(rows), rows)
+        top = window_rows(est_ref, left_ref[rows, :], right_ref[rows, :], rows)
         rows = slice(obs_first, obs_first + RADIUS)
-        low = window_rows(obs_ref, turn(left(rows)), turn(right(rows)), rows)
+        low = window_rows(obs_ref, turn(left_ref[rows, :]), turn(right_ref[rows, :]), rows)
         ends.append((top, low))
-    even = is_even(row_ref)
     for part, rows in ((0, slice(0, MARGIN)), (1, slice(MARGIN, HALO))):
-        even_ref[rows, :] = jnp.where(even, ends[1][part], ends[0][part])
-        odd_ref[rows, :] = jnp.where(even, ends[0][part], ends[1][part])
-
-
-def ordered(place_ref, even_ref, odd_ref):
-    even = is_even(place_ref)
-    before = lambda rows: jnp.where(even, odd_ref[rows, :], even_ref[rows, :])
-    after = lambda rows: jnp.where(even, even_ref[rows, :], odd_ref[rows, :])
-    return before, after
+        pair_ref[rows, :] = jnp.where(even, ends[1][part], ends[0][part])
+        outer_ref[rows, :] = jnp.where(even, ends[0][part], ends[1][part])
 
 
 def paired(top, low, near, far):
@@ -205,7 +193,7 @@
 
 
 def prepare_kernel(
-    est_ref, obs_ref, right_ref, left_ref, bank_ref, table_ref,
+    est_ref, obs_ref, left_ref, right_ref, bank_ref, table_ref,
     kern_ref, spec_ref, frame_ref,
     raw_ref, wide_ref, tall_ref, fold_ref, sums_ref,
 ):
@@ -269,28 +257,11 @@
     put_down(sin_ref, first, HALF, vr - ur, slice(LANES, BLOCK))
 
 
-def update_kernel(
-    member_ref, row_ref, col_ref, index_ref, cover_ref,
-    est_ref, frame_ref, end_even_ref, end_odd_ref, kern_ref, part_ref,
-    row_margin_ref, row_in_ref, row_out_ref, ready_ref, col_out_ref, col_back_ref,
-    out_ref,
-    fold_ref, sums_ref, spec_ref, cos0_ref, sin0_ref, cos1_ref, sin1_ref, mid0_ref, mid1_ref,
-    blur_ref, pick_ref, mask_ref,
+def maps_kernel(
+    member_ref, row_ref, col_ref, index_ref, cover_ref, pick_ref, mask_ref, own_ref, odd_ref, weight_ref
 ):
     member, tile_row, tile_col = member_ref[0], row_ref[0], col_ref[0]
     rows_of_tiles, cols_of_tiles, exposures = cover_ref.shape
-    col_in_ref = ready_ref.at[FRAME : FRAME + 2 * BLOCK, 0 : 2 * BLOCK]
-    grown = ((cos0_ref, sin0_ref), (cos1_ref, sin1_ref))
-    mids = (mid0_ref, mid1_ref)
-
-    above, below = ordered(row_ref, end_even_ref, end_odd_ref)
-    top = above(slice(0, MARGIN))
-    low = reverse(below(slice(0, MARGIN)))
-    put_across(fold_ref, slice(0, MARGIN), top - low)
-    put_across(fold_ref, slice(MARGIN, 2 * MARGIN), top + low)
-    analyse(fold_ref, 0, MARGIN, col_in_ref, sums_ref)
-    spectrum(row_margin_ref, sums_ref, MARGIN, spec_ref, part_ref)
-
     lane = lax.broadcasted_iota(jnp.int32, (RADIUS, FRAME), 1)
     for step, spans in ((-1, ((LANES, RADIUS),)), (0, ((0, LANES), (FOLD, LANES))), (1, ((FOLD + LANES, RADIUS),))):
         near = []
@@ -311,6 +282,46 @@
             for row in range(first, first + count, RADIUS):
                 pick_ref[row : row + RADIUS, :] = pick
                 mask_ref[row : row + RADIUS, :] = cover
+
+    covering = lax.fori_loop(0, exposures, lambda e, n: n + cover_ref[tile_row, tile_col, e], 0)
+    own_cover = cover_ref[tile_row, tile_col, member].astype(jnp.float32)
+    own_ref[...] = jnp.full(own_ref.shape, index_ref[tile_col, tile_row], jnp.int32)
+    odd_ref[...] = jnp.full(odd_ref.shape, lax.rem(tile_row, 2), jnp.int32)
+    weight_ref[...] = jnp.full(weight_ref.shape, own_cover, jnp.float32) / jnp.full(
+        weight_ref.shape, covering.astype(jnp.float32), jnp.float32
+    )
+
+
+def update_kernel(
+    pick_ref, mask_ref, own_ref, odd_ref, weight_ref,
+    est_ref, frame_ref, pair_ref, outer_ref, kern_ref, part_ref,
+    row_margin_ref, row_in_ref, row_out_ref, ready_ref, col_out_ref, col_back_ref,
+    out_ref,
+    fold_ref, sums_ref, spec_ref, cos0_ref, sin0_ref, cos1_ref, sin1_ref, mid0_ref, mid1_ref,
+    blur_ref, own_kern_ref,
+):
+    col_in_ref = ready_ref.at[FRAME : FRAME + 2 * BLOCK, 0 : 2 * BLOCK]
+    grown = ((cos0_ref, sin0_ref), (cos1_ref, sin1_ref))
+    mids = (mid0_ref, mid1_ref)
+
+    odd = odd_ref[0:1, :] != 0
+    above = jnp.where(odd, pair_ref[...], outer_ref[...])
+    below = jnp.where(odd, outer_ref[...], pair_ref[...])
+    top = above[0:MARGIN, :]
+    low = reverse(below[0:MARGIN, :])
+    put_across(fold_ref, slice(0, MARGIN), top - low)
+    put_across(fold_ref, slice(MARGIN, 2 * MARGIN), top + low)
+    analyse(fold_ref, 0, MARGIN, col_in_ref, sums_ref)
+    spectrum(row_margin_ref, sums_ref, MARGIN, spec_ref, part_ref)
+
+    own = own_ref[0:1, :]
+    for row in range(0, FRAME, 48):
+        rows = slice(row, row + 48)
+        for lanes in (slice(0, LANES), slice(LANES, BLOCK)):
+            chosen = kern_ref[0, rows, lanes]
+            for model in range(1, MODELS):
+                chosen = jnp.where(own == model, kern_ref[model, rows, lanes], chosen)
+            own_kern_ref[rows, lanes] = chosen
 
     def rows_back(block, count, step=None):
         cos_ref, sin_ref = grown[block]
@@ -323,17 +334,17 @@
         put_across(mids[block], slice(0, count), odd + even)
         put_across(mids[block], slice(count, 2 * count), odd - even)
 
-    def grow(model, block, sign):
+    def grow(kern, block, sign):
         def step(part):
             for first in range(part * HALF // 2, (part + 1) * HALF // 2, 48):
-                product(spec_ref, kern_ref.at[model], block, sign, grown[block], first, first + 48)
+                product(spec_ref, kern, block, sign, grown[block], first, first + 48)
 
         return step
 
     def forward(model, carry):
-        rows_back(0, FOLD, grow(model, 1, 1))
+        rows_back(0, FOLD, grow(kern_ref.at[model], 1, 1))
         later = jnp.minimum(model + 1, MODELS - 1)
-        rows_back(1, FOLD, grow(later, 0, 1))
+        rows_back(1, FOLD, grow(kern_ref.at[later], 0, 1))
         one, two = (
             matmul(
                 across3(mids[block], slice(0, REACH), 0, BLOCK, BLOCK),
@@ -349,8 +360,8 @@
             blur_ref[:, lanes] = jnp.where(pick_ref[:, lanes] == model, value, blur_ref[:, lanes])
         return carry
 
-    grow(0, 0, 1)(0)
-    grow(0, 0, 1)(1)
+    grow(kern_ref.at[0], 0, 1)(0)
+    grow(kern_ref.at[0], 0, 1)(1)
     lax.fori_loop(0, MODELS, forward, 0)
 
     def ratio(rows, values):
@@ -364,20 +375,17 @@
         low = ratio(slice(FOLD + row, FOLD + row + 64), frame_ref[LANES + row : LANES + row + 64, :])
         put_across(fold_ref, slice(row, row + 64), top - low)
         put_across(fold_ref, slice(HALF + row, HALF + row + 64), top + low)
-    top = ratio(slice(LANES, FOLD), above(slice(MARGIN, HALO)))
-    low = ratio(slice(FOLD + LANES, REACH), reverse(below(slice(MARGIN, HALO))))
+    top = ratio(slice(LANES, FOLD), above[MARGIN:HALO, :])
+    low = ratio(slice(FOLD + LANES, REACH), reverse(below[MARGIN:HALO, :]))
     put_across(fold_ref, slice(LANES, FOLD), top - low)
     put_across(fold_ref, slice(HALF + LANES, HALF + FOLD), top + low)
     analyse(fold_ref, 0, HALF, col_in_ref, sums_ref)
     spectrum(row_in_ref, sums_ref, HALF, spec_ref, None)
 
-    own_model = index_ref[tile_col, tile_row]
-    covering = lax.fori_loop(0, exposures, lambda e, n: n + cover_ref[tile_row, tile_col, e], 0)
-    own_cover = cover_ref[tile_row, tile_col, member].astype(jnp.float32)
-    weight = jnp.full((1, LANES), own_cover, jnp.float32) / jnp.full((1, LANES), covering.astype(jnp.float32), jnp.float32)
-    grow(own_model, 0, -1)(0)
-    grow(own_model, 0, -1)(1)
-    rows_back(0, LANES, grow(own_model, 1, -1))
+    weight = weight_ref[0:1, :]
+    grow(own_kern_ref, 0, -1)(0)
+    grow(own_kern_ref, 0, -1)(1)
+    rows_back(0, LANES, grow(own_kern_ref, 1, -1))
     rows_back(1, LANES)
     for block in range(2):
         own = slice(block * LANES, (block + 1) * LANES)
@@ -398,7 +406,7 @@
     return pltpu.VMEM(shape, jnp.bfloat16)
 
 
-def pack_ends(row, estimate, frame, side_even, side_odd):
+def pack_ends(row, estimate, frame, left, right):
     return pl.pallas_call(
         ends_kernel,
         out_shape=(f32(HALO, FRAME),) * 2,
@@ -406,10 +414,27 @@
         out_specs=(VMEM,) * 2,
         compiler_params=pltpu.CompilerParams(vmem_limit_bytes=4 << 20),
         name="pack_ends",
-    )(row, estimate, frame, side_even, side_odd)
-
-
-def prepare(estimate, frame, side_even, side_odd, bank, table):
+    )(row, estimate, frame, left, right)
+
+
+def pixel_maps(member, row, col, index, coverage):
+    whole = jax.ShapeDtypeStruct((REACH, FRAME), jnp.int32)
+    small = (8, LANES)
+    return pl.pallas_call(
+        maps_kernel,
+        out_shape=(
+            whole, whole, jax.ShapeDtypeStruct(small, jnp.int32),
+            jax.ShapeDtypeStruct((8, FRAME), jnp.int32), f32(*small),
+        ),
+        in_specs=[SMEM] * 5,
+        out_specs=(VMEM,) * 5,
+        compiler_params=pltpu.CompilerParams(vmem_limit_bytes=4 << 20),
+        cost_estimate=pl.CostEstimate(flops=1 << 28, bytes_accessed=1 << 20, transcendentals=0),
+        name="pixel_maps",
+    )(member, row, col, index, coverage)
+
+
+def prepare(estimate, frame, left, right, bank, table):
     return pl.pallas_call(
         prepare_kernel,
         out_shape=(f32(MODELS, FRAME, BLOCK), f32(FRAME, 2 * BLOCK), f32(TILE, FRAME)),
@@ -425,15 +450,15 @@
         compiler_params=pltpu.CompilerParams(vmem_limit_bytes=16 << 20),
         cost_estimate=pl.CostEstimate(flops=2 << 30, bytes_accessed=4 << 20, transcendentals=8192),
         name="prepare",
-    )(estimate, frame, side_even, side_odd, bank, table["ready"])
-
-
-def tile_update(member, row, col, index, coverage, estimate, frame, end_even, end_odd, spectra, part, table):
+    )(estimate, frame, left, right, bank, table["ready"])
+
+
+def tile_update(maps, estimate, frame, pair, outer, spectra, part, table):
     names = ("row_margin", "row_in", "row_out", "ready", "col_out", "col_back")
     return pl.pallas_call(
         update_kernel,
         out_shape=f32(TILE, TILE),
-        in_specs=[SMEM] * 5 + [VMEM] * 12,
+        in_specs=[VMEM] * 17,
         out_specs=VMEM,
         scratch_shapes=[
             half_scratch(FRAME, 2 * FRAME),
@@ -446,25 +471,29 @@
             half_scratch(REACH, 2 * BLOCK),
             half_scratch(REACH, 2 * BLOCK),
             pltpu.VMEM((REACH, FRAME), jnp.float32),
-            pltpu.VMEM((REACH, FRAME), jnp.int32),
-            pltpu.VMEM((REACH, FRAME), jnp.int32),
+            pltpu.VMEM((FRAME, BLOCK), jnp.float32),
         ],
         compiler_params=pltpu.CompilerParams(vmem_limit_bytes=20 << 20),
         cost_estimate=pl.CostEstimate(flops=4 << 30, bytes_accessed=8 << 20, transcendentals=0),
         name="tile_update",
     )(
-        member, row, col, index, coverage, estimate, frame, end_even, end_odd, spectra, part,
+        *maps, estimate, frame, pair, outer, spectra, part,
         *(table[name] for name in names),
     )
 
 
-def exchange(even, odd, axis):
+def exchange(first, last, axis):
+    upward = [(i, i + 1) for i in range(lax.axis_size(axis) - 1)]
+    after = lax.ppermute(first, axis, [(b, a) for a, b in upward])
+    return lax.ppermute(last, axis, upward), after
+
+
+def trade(pair, outer, axis):
     count = lax.axis_size(axis)
     swap = lambda first: [
         step for i in range(first, count - 1, 2) for step in ((i, i + 1), (i + 1, i))
     ]
-    near = lax.ppermute(even, axis, swap(0))
-    return near, lax.ppermute(odd, axis, swap(1))
+    return lax.ppermute(pair, axis, swap(0)), lax.ppermute(outer, axis, swap(1))
 
 
 def exposure_sum(block):
@@ -490,16 +519,11 @@
     own = estimate
     first = jnp.concatenate([frame[:, :MARGIN], own[:, :MARGIN]], axis=1)
     last = jnp.concatenate([own[:, TILE - MARGIN :], frame[:, TILE - MARGIN :]], axis=1)
-    upward = [(i, i + 1) for i in range(lax.axis_size("skyy") - 1)]
-    sides = (
-        lax.ppermute(first, "skyy", [(b, a) for a, b in upward]),
-        lax.ppermute(last, "skyy", upward),
-    )
-    ends = exchange(*pack_ends(row, own, frame, *sides), "skyx")
+    sides = exchange(first, last, "skyy")
+    maps = pixel_maps(member, row, col, index, cover)
+    ends = trade(*pack_ends(row, own, frame, *sides), "skyx")
     spectra, part, folded = prepare(own, frame, *sides, bank, table)
-    update = tile_update(
-        member, row, col, index, cover, own, folded, *ends, spectra, part, table
-    )
+    update = tile_update(maps, own, folded, *ends, spectra, part, table)
     return exposure_sum(update)
 
 

time: 74.4 us -> 73.4 us (0.987)
  waiting for transfers between devices: 8.88 us -> 7.83 us
    ppermute x4, waiting for transfers between devices: 6.88 us -> 5.83 us  [the longest x1 4.24 us: exchange(): after = lax.ppermute(first, axis, [(b, a) for a, b in upward])]
    pallas_call x1 -> x2, Pallas kernels: 7.59 us -> 7.68 us  [the longest x1 6.65 us: tile_update(): pl.pallas_call(update_kernel, out_shape=f32(TILE, TILE), in_specs=[VMEM]...]
  transfers between devices with their start and end apart: 5 -> 5, of which waited for: 4 -> 4; matrix products, arithmetic and copies ran while one was open for 0% -> 0% of each run, Pallas kernels for 2% -> 3%
where the time goes in v2:
time: 73.4 us; the launch traced here: 73.1 us
  blocking collectives  32.2 us (44%)
  starting transfers between devices  21.3 us (29%)
  Pallas kernels  9.19 us (13%)
  waiting for transfers between devices  7.83 us (11%)
  local copies, waits for them, and re-layouts  2.15 us (3%)
    all_to_all x1, blocking collectives, exposure_sum(): lax.all_to_all(block.reshape(near, rows // near, cols), 'exp_y', 0, 0)  18.4 us
    all_to_all x1, blocking collectives, exposure_sum(): return lax.all_to_all(spread, 'exp_y', 0, 0).reshape(rows, cols)  13.8 us
    ppermute x1, starting transfers between devices, exposure_sum(): piece = piece + lax.ppermute(piece, 'exp_z', [(0, 1), (1, 0)])  9.76 us
    pallas_call x1, Pallas kernels, tile_update(): pl.pallas_call(update_kernel, out_shape=f32(TILE, TILE), in_specs=[VMEM]...  6.65 us
    ppermute x1, starting transfers between devices, trade(): lax.ppermute(outer, axis, swap(1))  4.89 us
    ppermute x1, waiting for transfers between devices, exchange(): after = lax.ppermute(first, axis, [(b, a) for a, b in upward])  4.24 us
    ppermute x1, starting transfers between devices, exchange(): return (lax.ppermute(last, axis, upward), after)  3.4 us
    ppermute x1, waiting for transfers between devices, exposure_sum(): piece = piece + lax.ppermute(piece, 'exp_z', [(0, 1), (1, 0)])  2 us
  transfers between devices with their start and end apart: 5, of which 4 were waited for; matrix products, arithmetic and copies ran while one was open for 0% of the time, Pallas kernels for 3%

profile of v2, /device:TPU:64, one launch (start us, length us, event | category | flops | bytes accessed | tf_op | source)
XLA Modules:
  0.0 73.1 jit_solution(5599013076752018361)
XLA Ops:
  0.0 0.0 copy-start
  0.0 0.0 copy-start.1
  0.0 0.0 copy-start.4
  0.0 0.0 copy-start.3
  0.0 0.0 copy-start.2
  0.0 0.0 copy-start.5
  0.0 1.4 %fusion = (f32[256,64]{1,0:T(8,128)S(1)}, f32[256,64]{1,0:T(8,128)S(1)}, f32[256,64]{1,0:T(8,128)S(1)}, f32[256,64]{1,0:T(8,128)S(1)}) fusion(f32[256,256]{1,0:T(8,128)} %bitcast.13, f32[256,256]{1,0:T(8,128)} %est_ref.5), kind=kLoop, calls=%fused_computation.2 | loop fusion | bytes 524288 | tf_op jit(solution)/shard_map/slice | solution.py:520
  1.4 0.1 pad_maximum_fusion
  1.5 3.4 %collective-permute-start = (f32[256,128]{1,0:T(8,128)S(1)}, f32[256,128]{1,0:T(8,128)S(1)}, u32[]{:S(2)}, u32[]{:S(2)}) collective-permute-start(f32[256,128]{1,0:T(8,128)S(1)} %pad_maximum_fusion), channel_id=1, source_target_pairs={{0,1},{1,2},{2,3},{4,5},{5,6},{6,7},{8,9},{9,10},{10,11},{12,13},{... | collective-permute-start | bytes 393224 | tf_op jit(solution)/shard_map/ppermute | solution.py:488
  4.9 0.1 pad_maximum_fusion.1
  5.0 1.3 %collective-permute-start.1 = (f32[256,128]{1,0:T(8,128)S(1)}, f32[256,128]{1,0:T(8,128)S(1)}, u32[]{:S(2)}, u32[]{:S(2)}) collective-permute-start(f32[256,128]{1,0:T(8,128)S(1)} %pad_maximum_fusion.1), channel_id=1, source_target_pairs={{1,0},{2,1},{3,2},{5,4},{6,5},{7,6},{9,8},{10,9},{11,10},{13,12},{... | collective-permute-start | bytes 393224 | tf_op jit(solution)/shard_map/ppermute | solution.py:487
  6.4 0.0 copy-done.4
  6.4 0.0 copy-done.3
  6.4 1.0 %pixel_maps.1 = (s32[320,384]{1,0:T(8,128)S(1)}, s32[320,384]{1,0:T(8,128)S(1)}, s32[8,128]{1,0:T(8,128)S(1)}, s32[8,384]{1,0:T(8,128)S(1)}, f32[8,128]{1,0:T(8,128)S(1)}) custom-call(s32[1]{0:T(128)} %bitcast.member_ref, s32[1]{0:T(128)} %bitcast.1.row_ref, s32[1]{0:T(128)} %bitcast.2.col_ref, s32[4,8]{1,0:T(4,128)S(1)} %bitcast.19, s32[8,4,16]{2,1,0:T(4,128)S(1)} %bitcast.18), custom_call_target="tpu_custom_call" | custom-call | flops 268435456 | bytes 1048576 | tf_op jit(solution)/shard_map/pixel_maps/pallas_call | solution.py:423
  7.4 0.2 collective-permute-done.left_ref
  7.7 4.2 %collective-permute-done.1.right_ref = f32[256,128]{1,0:T(8,128)S(1)} collective-permute-done((f32[256,128]{1,0:T(8,128)S(1)}, f32[256,128]{1,0:T(8,128)S(1)}, u32[]{:S(2)}, u32[]{:S(2)}) %collective-permute-start.1) | collective-permute-done | bytes 131104 | tf_op jit(solution)/shard_map/ppermute | solution.py:487
  11.9 0.0 copy-done
  11.9 0.0 copy-done.1
  11.9 0.1 pack_ends.1
  12.1 1.9 %collective-permute-start.2 = (f32[96,384]{1,0:T(8,128)S(1)}, f32[96,384]{1,0:T(8,128)S(1)}, u32[]{:S(2)}, u32[]{:S(2)}) collective-permute-start(f32[96,384]{1,0:T(8,128)S(1)} %get-tuple-element.21), channel_id=1, source_target_pairs={{0,4},{4,0},{8,12},{12,8},{16,20},{20,16},{24,28},{28,24},{1,5},{5... | collective-permute-start | bytes 442376 | tf_op jit(solution)/shard_map/ppermute | solution.py:496
  14.0 4.9 %collective-permute-start.3 = (f32[96,384]{1,0:T(8,128)S(1)}, f32[96,384]{1,0:T(8,128)S(1)}, u32[]{:S(2)}, u32[]{:S(2)}) collective-permute-start(f32[96,384]{1,0:T(8,128)S(1)} %get-tuple-element.22), channel_id=1, source_target_pairs={{4,8},{8,4},{12,16},{16,12},{20,24},{24,20},{5,9},{9,5},{13,17},{1... | collective-permute-start | bytes 442376 | tf_op jit(solution)/shard_map/ppermute | solution.py:496
  18.9 0.0 copy-done.2
  18.9 0.0 copy-done.5
  18.9 0.0 copy-start.6
  18.9 0.0 copy-start.7
  18.9 0.0 copy-start.8
  18.9 0.0 copy-start.9
  19.0 0.0 copy-start.10
  19.0 1.4 %prepare.1 = (f32[4,384,256]{2,1,0:T(8,128)S(1)}, f32[384,512]{1,0:T(8,128)S(1)}, f32[256,384]{1,0:T(8,128)S(1)}) custom-call(f32[256,256]{1,0:T(8,128)S(1)} %copy-done.1, f32[256,256]{1,0:T(8,128)S(1)} %bitcast.15, f32[256,128]{1,0:T(8,128)S(1)} %collective-permute-done.left_ref, f32[256,128]{1,0:T(8,128)S(1)} %collective-permute-done.1.right_ref, ...), custom_call_target="tpu_custom_call" | custom-call | flops 2147483648 | bytes 4194304 | tf_op jit(solution)/shard_map/prepare/pallas_call | solution.py:438
  20.3 0.0 collective-permute-done.2.pair_ref
  20.4 1.3 %collective-permute-done.3.outer_ref = f32[96,384]{1,0:T(8,128)S(1)} collective-permute-done((f32[96,384]{1,0:T(8,128)S(1)}, f32[96,384]{1,0:T(8,128)S(1)}, u32[]{:S(2)}, u32[]{:S(2)}) %collective-permute-start.3) | collective-permute-done | bytes 147488 | tf_op jit(solution)/shard_map/ppermute | solution.py:496
  21.7 0.0 copy-done.6
  21.7 0.0 copy-done.7
  21.7 0.0 copy-done.8
  21.7 0.0 copy-done.9
  21.7 0.0 copy-done.10
  21.7 6.6 %tile_update.1 = f32[256,256]{1,0:T(8,128)S(1)} custom-call(s32[320,384]{1,0:T(8,128)S(1)} %get-tuple-element.15.pick_ref, s32[320,384]{1,0:T(8,128)S(1)} %get-tuple-element.16.mask_ref, s32[8,128]{1,0:T(8,128)S(1)} %get-tuple-element.17.own_ref, s32[8,384]{1,0:T(8,128)S(1)} %get-tuple-element.18.odd_ref, f32[8,128]{1,0:T(8,128)S(1)} %get-tuple-element.19.weight_ref, ...), custom_call_target="tpu_custom_call" | custom-call | flops 4294967296 | bytes 8388608 | tf_op jit(solution)/shard_map/tile_update/pallas_call | solution.py:458
  28.4 18.4 %all_to_all.10 = f32[8,32,256]{2,1,0:T(8,128)S(1)} all-to-all(f32[8,32,256]{2,1,0:T(8,128)S(1)} %bitcast.16), channel_id=1, replica_groups=mesh['exp_y'=8,'exp_z'=2,'skyx'=8,'skyy'=4] {'exp_y'}, dimensions={0} | all-to-all | bytes 524288 | tf_op jit(solution)/shard_map/all_to_all | solution.py:502
  46.8 9.8 %collective-permute-start.4 = (f32[32,256]{1,0:T(8,128)S(1)}, f32[32,256]{1,0:T(8,128)S(1)}, u32[]{:S(2)}, u32[]{:S(2)}) collective-permute-start(f32[32,256]{1,0:T(8,128)S(1)} %reduce_sum.9), channel_id=1, source_target_pairs={{0,32},{32,0},{1,33},{33,1},{2,34},{34,2},{3,35},{35,3},{4,36},{36... | collective-permute-start | bytes 98312 | tf_op jit(solution)/shard_map/ppermute | solution.py:504
  56.6 2.0 %collective-permute-done.4 = f32[32,256]{1,0:T(8,128)S(1)} collective-permute-done((f32[32,256]{1,0:T(8,128)S(1)}, f32[32,256]{1,0:T(8,128)S(1)}, u32[]{:S(2)}, u32[]{:S(2)}) %collective-permute-start.4) | collective-permute-done | bytes 32800 | tf_op jit(solution)/shard_map/ppermute | solution.py:504
  58.6 13.8 %all_to_all.11 = f32[8,32,256]{2,1,0:T(8,128)S(1)} all-to-all(f32[8,32,256]{2,1,0:T(8,128)S(1)} %broadcast_in_dim.2), channel_id=1, replica_groups=mesh['exp_y'=8,'exp_z'=2,'skyx'=8,'skyy'=4] {'exp_y'}, dimensions={0} | all-to-all | bytes 524288 | tf_op jit(solution)/shard_map/all_to_all | solution.py:506
  72.4 0.7 copy.13
  (3 shorter events, 0.0 us)
Async XLA Ops:
  0.0 11.9 %copy-start = (f32[1,256,256]{2,1,0:T(8,128)S(1)}, f32[1,256,256]{2,1,0:T(8,128)}, u32[]{:S(2)}) copy-start(f32[1,256,256]{2,1,0:T(8,128)} %param.12) | copy-start | bytes 786436
  0.0 11.9 %copy-start.1 = (f32[256,256]{1,0:T(8,128)S(1)}, f32[256,256]{1,0:T(8,128)}, u32[]{:S(2)}) copy-start(f32[256,256]{1,0:T(8,128)} %est_ref.5) | copy-start | bytes 786436
  0.0 6.3 %copy-start.4 = (s32[1,8,4]{1,2,0:T(4,128)S(1)}, s32[1,8,4]{1,2,0:T(4,128)}, u32[]{:S(2)}) copy-start(s32[1,8,4]{1,2,0:T(4,128)} %param.14) | copy-start | bytes 388
  0.0 6.4 %copy-start.3 = (s32[16,8,4]{0,2,1:T(4,128)S(1)}, s32[16,8,4]{0,2,1:T(4,128)}, u32[]{:S(2)}) copy-start(s32[16,8,4]{0,2,1:T(4,128)} %param.15) | copy-start | bytes 6148
  0.0 18.9 %copy-start.2 = (f32[1,4,65,65]{3,1,2,0:T(4,128)S(1)}, f32[1,4,65,65]{3,1,2,0:T(4,128)}, u32[]{:S(2)}) copy-start(f32[1,4,65,65]{3,1,2,0:T(4,128)} %param.13) | copy-start | bytes 202804
  0.0 18.9 %copy-start.5 = (bf16[1152,640]{1,0:T(8,128)(2,1)S(1)}, bf16[1152,640]{1,0:T(8,128)(2,1)}, u32[]{:S(2)}) copy-start(bf16[1152,640]{1,0:T(8,128)(2,1)} %constant.35.clone.table_ref.ready_ref) | copy-start | bytes 4423684
  1.5 6.1 %collective-permute-start = (f32[256,128]{1,0:T(8,128)S(1)}, f32[256,128]{1,0:T(8,128)S(1)}, u32[]{:S(2)}, u32[]{:S(2)}) collective-permute-start(f32[256,128]{1,0:T(8,128)S(1)} %pad_maximum_fusion), channel_id=1, source_target_pairs={{0,1},{1,2},{2,3},{4,5},{5,6},{6,7},{8,9},{9,10},{10,11},{12,13},{... | collective-permute-start | bytes 393224 | tf_op jit(solution)/shard_map/ppermute | solution.py:488
  5.0 6.9 %collective-permute-start.1 = (f32[256,128]{1,0:T(8,128)S(1)}, f32[256,128]{1,0:T(8,128)S(1)}, u32[]{:S(2)}, u32[]{:S(2)}) collective-permute-start(f32[256,128]{1,0:T(8,128)S(1)} %pad_maximum_fusion.1), channel_id=1, source_target_pairs={{1,0},{2,1},{3,2},{5,4},{6,5},{7,6},{9,8},{10,9},{11,10},{13,12},{... | collective-permute-start | bytes 393224 | tf_op jit(solution)/shard_map/ppermute | solution.py:487
  12.1 8.3 %collective-permute-start.2 = (f32[96,384]{1,0:T(8,128)S(1)}, f32[96,384]{1,0:T(8,128)S(1)}, u32[]{:S(2)}, u32[]{:S(2)}) collective-permute-start(f32[96,384]{1,0:T(8,128)S(1)} %get-tuple-element.21), channel_id=1, source_target_pairs={{0,4},{4,0},{8,12},{12,8},{16,20},{20,16},{24,28},{28,24},{1,5},{5... | collective-permute-start | bytes 442376 | tf_op jit(solution)/shard_map/ppermute | solution.py:496
  14.0 7.7 %collective-permute-start.3 = (f32[96,384]{1,0:T(8,128)S(1)}, f32[96,384]{1,0:T(8,128)S(1)}, u32[]{:S(2)}, u32[]{:S(2)}) collective-permute-start(f32[96,384]{1,0:T(8,128)S(1)} %get-tuple-element.22), channel_id=1, source_target_pairs={{4,8},{8,4},{12,16},{16,12},{20,24},{24,20},{5,9},{9,5},{13,17},{1... | collective-permute-start | bytes 442376 | tf_op jit(solution)/shard_map/ppermute | solution.py:496
  18.9 2.8 %copy-start.6 = (bf16[512,512]{1,0:T(8,128)(2,1)S(1)}, bf16[512,512]{1,0:T(8,128)(2,1)}, u32[]{:S(2)}) copy-start(bf16[512,512]{1,0:T(8,128)(2,1)} %constant.39.clone.col_out_ref) | copy-start | bytes 1572868
  18.9 2.8 %copy-start.7 = (bf16[384,576]{1,0:T(8,128)(2,1)S(1)}, bf16[384,576]{1,0:T(8,128)(2,1)}, u32[]{:S(2)}) copy-start(bf16[384,576]{1,0:T(8,128)(2,1)} %constant.37.clone.row_in_ref) | copy-start | bytes 1327108
  18.9 2.8 %copy-start.8 = (bf16[320,576]{1,0:T(8,128)(2,1)S(1)}, bf16[320,576]{1,0:T(8,128)(2,1)}, u32[]{:S(2)}) copy-start(bf16[320,576]{1,0:T(8,128)(2,1)} %constant.38.clone.row_out_ref) | copy-start | bytes 1105924
  18.9 2.8 %copy-start.9 = (bf16[512,256]{1,0:T(8,128)(2,1)S(1)}, bf16[512,256]{1,0:T(8,128)(2,1)}, u32[]{:S(2)}) copy-start(bf16[512,256]{1,0:T(8,128)(2,1)} %constant.40.clone.col_back_ref) | copy-start | bytes 786436
  19.0 2.8 %copy-start.10 = (bf16[384,192]{1,0:T(8,128)(2,1)S(1)}, bf16[384,192]{1,0:T(8,128)(2,1)}, u32[]{:S(2)}) copy-start(bf16[384,192]{1,0:T(8,128)(2,1)} %constant.36.clone.row_margin_ref) | copy-start | bytes 442372
  46.8 11.8 %collective-permute-start.4 = (f32[32,256]{1,0:T(8,128)S(1)}, f32[32,256]{1,0:T(8,128)S(1)}, u32[]{:S(2)}, u32[]{:S(2)}) collective-permute-start(f32[32,256]{1,0:T(8,128)S(1)} %reduce_sum.9), channel_id=1, source_target_pairs={{0,32},{32,0},{1,33},{33,1},{2,34},{34,2},{3,35},{35,3},{4,36},{36... | collective-permute-start | bytes 98312 | tf_op jit(solution)/shard_map/ppermute | solution.py:504

commit v3 on v2

--- a/solution.py
+++ b/solution.py
@@ -46,7 +46,6 @@
     starts = (-MARGIN, TILE // 2 - RADIUS)
     column_in = []
     column_out = []
-    column_back = []
     for block, start in enumerate(starts):
         column = np.arange(BLOCK) + block * LANES - MARGIN
         place = column - start
@@ -55,7 +54,6 @@
         first, last = (-RADIUS, LANES) if block == 0 else (LANES, TILE + RADIUS)
         wanted = (column >= first) & (column < last)
         column_out.append(waves(place, BLOCK) * wanted[None, :])
-        column_back.append(waves(np.arange(LANES) + block * LANES - start, BLOCK))
     offsets = np.arange(LANES) - RADIUS
     inside = offsets <= RADIUS
     kernel_rows = (waves(offsets, FRAME) * inside[None, :])[:, :DEPTH]
@@ -84,7 +82,6 @@
         "row_in": both(every),
         "row_out": both(np.concatenate([own, near]), lambda t: t.T),
         "col_out": pair(np.concatenate(column_out, axis=1)),
-        "col_back": pair(np.concatenate(column_back, axis=1)),
     }
 
 
@@ -295,10 +292,10 @@
 def update_kernel(
     pick_ref, mask_ref, own_ref, odd_ref, weight_ref,
     est_ref, frame_ref, pair_ref, outer_ref, kern_ref, part_ref,
-    row_margin_ref, row_in_ref, row_out_ref, ready_ref, col_out_ref, col_back_ref,
+    row_margin_ref, row_in_ref, row_out_ref, ready_ref, col_out_ref,
     out_ref,
     fold_ref, sums_ref, spec_ref, cos0_ref, sin0_ref, cos1_ref, sin1_ref, mid0_ref, mid1_ref,
-    blur_ref, own_kern_ref,
+    blur_ref, own_kern_ref, edge_ref,
 ):
     col_in_ref = ready_ref.at[FRAME : FRAME + 2 * BLOCK, 0 : 2 * BLOCK]
     grown = ((cos0_ref, sin0_ref), (cos1_ref, sin1_ref))
@@ -341,28 +338,29 @@
 
         return step
 
-    def forward(model, carry):
+    def columns_back(block):
+        return matmul(
+            across3(mids[block], slice(0, REACH), 0, BLOCK, BLOCK),
+            table3(col_out_ref, slice(block * BLOCK, (block + 1) * BLOCK)),
+        )
+
+    def keep(lanes, value, model):
+        blur_ref[:, lanes] = jnp.where(pick_ref[:, lanes] == model, value, blur_ref[:, lanes])
+
+    def forward(model):
         rows_back(0, FOLD, grow(kern_ref.at[model], 1, 1))
-        later = jnp.minimum(model + 1, MODELS - 1)
-        rows_back(1, FOLD, grow(kern_ref.at[later], 0, 1))
-        one, two = (
-            matmul(
-                across3(mids[block], slice(0, REACH), 0, BLOCK, BLOCK),
-                table3(col_out_ref, slice(block * BLOCK, (block + 1) * BLOCK)),
-            )
-            for block in range(2)
-        )
-        for lanes, value in (
-            (slice(0, LANES), one[:, 0:LANES]),
-            (slice(LANES, BLOCK), one[:, LANES:BLOCK] + two[:, 0:LANES]),
-            (slice(BLOCK, FRAME), two[:, LANES:BLOCK]),
-        ):
-            blur_ref[:, lanes] = jnp.where(pick_ref[:, lanes] == model, value, blur_ref[:, lanes])
-        return carry
+        one = columns_back(0)
+        keep(slice(0, LANES), one[:, 0:LANES], model)
+        edge_ref[...] = one[:, LANES:BLOCK]
+        rows_back(1, FOLD, grow(kern_ref.at[model + 1], 0, 1) if model + 1 < MODELS else None)
+        two = columns_back(1)
+        keep(slice(LANES, BLOCK), edge_ref[...] + two[:, 0:LANES], model)
+        keep(slice(BLOCK, FRAME), two[:, LANES:BLOCK], model)
 
     grow(kern_ref.at[0], 0, 1)(0)
     grow(kern_ref.at[0], 0, 1)(1)
-    lax.fori_loop(0, MODELS, forward, 0)
+    for model in range(MODELS):
+        forward(model)
 
     def ratio(rows, values):
         return jnp.where(mask_ref[rows, :] != 0, values / blur_ref[rows, :], 0.0)
@@ -389,7 +387,7 @@
     rows_back(1, LANES)
     for block in range(2):
         own = slice(block * LANES, (block + 1) * LANES)
-        back = matmul(across3(mids[block], slice(0, TILE), 0, BLOCK, BLOCK), table3(col_back_ref, own)) * weight
+        back = matmul(across3(mids[block], slice(0, TILE), 0, BLOCK, BLOCK), table3(col_out_ref, slice(block * BLOCK + MARGIN, block * BLOCK + MARGIN + LANES))) * weight
         out_ref[0:LANES, own] = est_ref[0:LANES, own] * back[0:LANES, :]
         out_ref[LANES:TILE, own] = est_ref[LANES:TILE, own] * reverse(back[LANES:TILE, :])
 
@@ -454,11 +452,11 @@
 
 
 def tile_update(maps, estimate, frame, pair, outer, spectra, part, table):
-    names = ("row_margin", "row_in", "row_out", "ready", "col_out", "col_back")
+    names = ("row_margin", "row_in", "row_out", "ready", "col_out")
     return pl.pallas_call(
         update_kernel,
         out_shape=f32(TILE, TILE),
-        in_specs=[VMEM] * 17,
+        in_specs=[VMEM] * 16,
         out_specs=VMEM,
         scratch_shapes=[
             half_scratch(FRAME, 2 * FRAME),
@@ -472,6 +470,7 @@
             half_scratch(REACH, 2 * BLOCK),
             pltpu.VMEM((REACH, FRAME), jnp.float32),
             pltpu.VMEM((FRAME, BLOCK), jnp.float32),
+            pltpu.VMEM((REACH, LANES), jnp.float32),
         ],
         compiler_params=pltpu.CompilerParams(vmem_limit_bytes=20 << 20),
         cost_estimate=pl.CostEstimate(flops=4 << 30, bytes_accessed=8 << 20, transcendentals=0),

time: 73.4 us -> 72.9 us (level)
  no operation moved by 1% of the time
where the time goes in v3:
time: 72.9 us; the launch traced here: 72.6 us
  blocking collectives  32.2 us (44%)
  starting transfers between devices  21.3 us (29%)
  Pallas kernels  8.65 us (12%)
  waiting for transfers between devices  7.84 us (11%)
  local copies, waits for them, and re-layouts  2.14 us (3%)
    all_to_all x1, blocking collectives, exposure_sum(): lax.all_to_all(block.reshape(near, rows // near, cols), 'exp_y', 0, 0)  18.4 us
    all_to_all x1, blocking collectives, exposure_sum(): return lax.all_to_all(spread, 'exp_y', 0, 0).reshape(rows, cols)  13.8 us
    ppermute x1, starting transfers between devices, exposure_sum(): piece = piece + lax.ppermute(piece, 'exp_z', [(0, 1), (1, 0)])  9.77 us
    pallas_call x1, Pallas kernels, tile_update(): pl.pallas_call(update_kernel, out_shape=f32(TILE, TILE), in_specs=[VMEM]...  6.11 us
    ppermute x1, starting transfers between devices, trade(): lax.ppermute(outer, axis, swap(1))  4.89 us
    ppermute x1, waiting for transfers between devices, exchange(): after = lax.ppermute(first, axis, [(b, a) for a, b in upward])  4.24 us
    ppermute x1, starting transfers between devices, exchange(): return (lax.ppermute(last, axis, upward), after)  3.4 us
    ppermute x1, waiting for transfers between devices, exposure_sum(): piece = piece + lax.ppermute(piece, 'exp_z', [(0, 1), (1, 0)])  2 us
  transfers between devices with their start and end apart: 5, of which 4 were waited for; matrix products, arithmetic and copies ran while one was open for 0% of the time, Pallas kernels for 3%

profile of v3, /device:TPU:64, one launch (start us, length us, event | category | flops | bytes accessed | tf_op | source)
XLA Modules:
  0.0 72.6 jit_solution(16193761618557278987)
XLA Ops:
  0.0 0.0 copy-start
  0.0 0.0 copy-start.1
  0.0 0.0 copy-start.4
  0.0 0.0 copy-start.3
  0.0 0.0 copy-start.2
  0.0 0.0 copy-start.5
  0.0 1.4 %fusion = (f32[256,64]{1,0:T(8,128)S(1)}, f32[256,64]{1,0:T(8,128)S(1)}, f32[256,64]{1,0:T(8,128)S(1)}, f32[256,64]{1,0:T(8,128)S(1)}) fusion(f32[256,256]{1,0:T(8,128)} %bitcast.13, f32[256,256]{1,0:T(8,128)} %est_ref.5), kind=kLoop, calls=%fused_computation.2 | loop fusion | bytes 524288 | tf_op jit(solution)/shard_map/slice | solution.py:519
  1.4 0.1 pad_maximum_fusion
  1.5 3.4 %collective-permute-start = (f32[256,128]{1,0:T(8,128)S(1)}, f32[256,128]{1,0:T(8,128)S(1)}, u32[]{:S(2)}, u32[]{:S(2)}) collective-permute-start(f32[256,128]{1,0:T(8,128)S(1)} %pad_maximum_fusion), channel_id=1, source_target_pairs={{0,1},{1,2},{2,3},{4,5},{5,6},{6,7},{8,9},{9,10},{10,11},{12,13},{... | collective-permute-start | bytes 393224 | tf_op jit(solution)/shard_map/ppermute | solution.py:487
  4.9 0.1 pad_maximum_fusion.1
  5.0 1.3 %collective-permute-start.1 = (f32[256,128]{1,0:T(8,128)S(1)}, f32[256,128]{1,0:T(8,128)S(1)}, u32[]{:S(2)}, u32[]{:S(2)}) collective-permute-start(f32[256,128]{1,0:T(8,128)S(1)} %pad_maximum_fusion.1), channel_id=1, source_target_pairs={{1,0},{2,1},{3,2},{5,4},{6,5},{7,6},{9,8},{10,9},{11,10},{13,12},{... | collective-permute-start | bytes 393224 | tf_op jit(solution)/shard_map/ppermute | solution.py:486
  6.4 0.0 copy-done.4
  6.4 0.0 copy-done.3
  6.4 1.0 %pixel_maps.1 = (s32[320,384]{1,0:T(8,128)S(1)}, s32[320,384]{1,0:T(8,128)S(1)}, s32[8,128]{1,0:T(8,128)S(1)}, s32[8,384]{1,0:T(8,128)S(1)}, f32[8,128]{1,0:T(8,128)S(1)}) custom-call(s32[1]{0:T(128)} %bitcast.member_ref, s32[1]{0:T(128)} %bitcast.1.row_ref, s32[1]{0:T(128)} %bitcast.2.col_ref, s32[4,8]{1,0:T(4,128)S(1)} %bitcast.19, s32[8,4,16]{2,1,0:T(4,128)S(1)} %bitcast.18), custom_call_target="tpu_custom_call" | custom-call | flops 268435456 | bytes 1048576 | tf_op jit(solution)/shard_map/pixel_maps/pallas_call | solution.py:421
  7.4 0.2 collective-permute-done.left_ref
  7.7 4.2 %collective-permute-done.1.right_ref = f32[256,128]{1,0:T(8,128)S(1)} collective-permute-done((f32[256,128]{1,0:T(8,128)S(1)}, f32[256,128]{1,0:T(8,128)S(1)}, u32[]{:S(2)}, u32[]{:S(2)}) %collective-permute-start.1) | collective-permute-done | bytes 131104 | tf_op jit(solution)/shard_map/ppermute | solution.py:486
  11.9 0.0 copy-done
  11.9 0.0 copy-done.1
  11.9 0.1 pack_ends.1
  12.1 1.9 %collective-permute-start.2 = (f32[96,384]{1,0:T(8,128)S(1)}, f32[96,384]{1,0:T(8,128)S(1)}, u32[]{:S(2)}, u32[]{:S(2)}) collective-permute-start(f32[96,384]{1,0:T(8,128)S(1)} %get-tuple-element.21), channel_id=1, source_target_pairs={{0,4},{4,0},{8,12},{12,8},{16,20},{20,16},{24,28},{28,24},{1,5},{5... | collective-permute-start | bytes 442376 | tf_op jit(solution)/shard_map/ppermute | solution.py:495
  14.0 4.9 %collective-permute-start.3 = (f32[96,384]{1,0:T(8,128)S(1)}, f32[96,384]{1,0:T(8,128)S(1)}, u32[]{:S(2)}, u32[]{:S(2)}) collective-permute-start(f32[96,384]{1,0:T(8,128)S(1)} %get-tuple-element.22), channel_id=1, source_target_pairs={{4,8},{8,4},{12,16},{16,12},{20,24},{24,20},{5,9},{9,5},{13,17},{1... | collective-permute-start | bytes 442376 | tf_op jit(solution)/shard_map/ppermute | solution.py:495
  18.9 0.0 copy-done.2
  18.9 0.0 copy-done.5
  18.9 0.0 copy-start.6
  18.9 0.0 copy-start.7
  18.9 0.0 copy-start.8
  18.9 0.0 copy-start.9
  19.0 1.4 %prepare.1 = (f32[4,384,256]{2,1,0:T(8,128)S(1)}, f32[384,512]{1,0:T(8,128)S(1)}, f32[256,384]{1,0:T(8,128)S(1)}) custom-call(f32[256,256]{1,0:T(8,128)S(1)} %copy-done.1, f32[256,256]{1,0:T(8,128)S(1)} %bitcast.15, f32[256,128]{1,0:T(8,128)S(1)} %collective-permute-done.left_ref, f32[256,128]{1,0:T(8,128)S(1)} %collective-permute-done.1.right_ref, ...), custom_call_target="tpu_custom_call" | custom-call | flops 2147483648 | bytes 4194304 | tf_op jit(solution)/shard_map/prepare/pallas_call | solution.py:436
  20.3 0.0 collective-permute-done.2.pair_ref
  20.3 1.4 %collective-permute-done.3.outer_ref = f32[96,384]{1,0:T(8,128)S(1)} collective-permute-done((f32[96,384]{1,0:T(8,128)S(1)}, f32[96,384]{1,0:T(8,128)S(1)}, u32[]{:S(2)}, u32[]{:S(2)}) %collective-permute-start.3) | collective-permute-done | bytes 147488 | tf_op jit(solution)/shard_map/ppermute | solution.py:495
  21.7 0.0 copy-done.6
  21.7 0.0 copy-done.7
  21.7 0.0 copy-done.8
  21.7 0.0 copy-done.9
  21.7 6.1 %tile_update.1 = f32[256,256]{1,0:T(8,128)S(1)} custom-call(s32[320,384]{1,0:T(8,128)S(1)} %get-tuple-element.15.pick_ref, s32[320,384]{1,0:T(8,128)S(1)} %get-tuple-element.16.mask_ref, s32[8,128]{1,0:T(8,128)S(1)} %get-tuple-element.17.own_ref, s32[8,384]{1,0:T(8,128)S(1)} %get-tuple-element.18.odd_ref, f32[8,128]{1,0:T(8,128)S(1)} %get-tuple-element.19.weight_ref, ...), custom_call_target="tpu_custom_call" | custom-call | flops 4294967296 | bytes 8388608 | tf_op jit(solution)/shard_map/tile_update/pallas_call | solution.py:456
  27.8 18.4 %all_to_all.10 = f32[8,32,256]{2,1,0:T(8,128)S(1)} all-to-all(f32[8,32,256]{2,1,0:T(8,128)S(1)} %bitcast.16), channel_id=1, replica_groups=mesh['exp_y'=8,'exp_z'=2,'skyx'=8,'skyy'=4] {'exp_y'}, dimensions={0} | all-to-all | bytes 524288 | tf_op jit(solution)/shard_map/all_to_all | solution.py:501
  46.3 9.8 %collective-permute-start.4 = (f32[32,256]{1,0:T(8,128)S(1)}, f32[32,256]{1,0:T(8,128)S(1)}, u32[]{:S(2)}, u32[]{:S(2)}) collective-permute-start(f32[32,256]{1,0:T(8,128)S(1)} %reduce_sum.9), channel_id=1, source_target_pairs={{0,32},{32,0},{1,33},{33,1},{2,34},{34,2},{3,35},{35,3},{4,36},{36... | collective-permute-start | bytes 98312 | tf_op jit(solution)/shard_map/ppermute | solution.py:503
  56.1 2.0 %collective-permute-done.4 = f32[32,256]{1,0:T(8,128)S(1)} collective-permute-done((f32[32,256]{1,0:T(8,128)S(1)}, f32[32,256]{1,0:T(8,128)S(1)}, u32[]{:S(2)}, u32[]{:S(2)}) %collective-permute-start.4) | collective-permute-done | bytes 32800 | tf_op jit(solution)/shard_map/ppermute | solution.py:503
  58.1 13.8 %all_to_all.11 = f32[8,32,256]{2,1,0:T(8,128)S(1)} all-to-all(f32[8,32,256]{2,1,0:T(8,128)S(1)} %broadcast_in_dim.2), channel_id=1, replica_groups=mesh['exp_y'=8,'exp_z'=2,'skyx'=8,'skyy'=4] {'exp_y'}, dimensions={0} | all-to-all | bytes 524288 | tf_op jit(solution)/shard_map/all_to_all | solution.py:505
  71.9 0.7 copy.12
  (3 shorter events, 0.0 us)
Async XLA Ops:
  0.0 11.9 %copy-start = (f32[1,256,256]{2,1,0:T(8,128)S(1)}, f32[1,256,256]{2,1,0:T(8,128)}, u32[]{:S(2)}) copy-start(f32[1,256,256]{2,1,0:T(8,128)} %param.11) | copy-start | bytes 786436
  0.0 11.9 %copy-start.1 = (f32[256,256]{1,0:T(8,128)S(1)}, f32[256,256]{1,0:T(8,128)}, u32[]{:S(2)}) copy-start(f32[256,256]{1,0:T(8,128)} %est_ref.5) | copy-start | bytes 786436
  0.0 6.3 %copy-start.4 = (s32[1,8,4]{1,2,0:T(4,128)S(1)}, s32[1,8,4]{1,2,0:T(4,128)}, u32[]{:S(2)}) copy-start(s32[1,8,4]{1,2,0:T(4,128)} %param.13) | copy-start | bytes 388
  0.0 6.4 %copy-start.3 = (s32[16,8,4]{0,2,1:T(4,128)S(1)}, s32[16,8,4]{0,2,1:T(4,128)}, u32[]{:S(2)}) copy-start(s32[16,8,4]{0,2,1:T(4,128)} %param.14) | copy-start | bytes 6148
  0.0 18.9 %copy-start.2 = (f32[1,4,65,65]{3,1,2,0:T(4,128)S(1)}, f32[1,4,65,65]{3,1,2,0:T(4,128)}, u32[]{:S(2)}) copy-start(f32[1,4,65,65]{3,1,2,0:T(4,128)} %param.12) | copy-start | bytes 202804
  0.0 18.9 %copy-start.5 = (bf16[1152,640]{1,0:T(8,128)(2,1)S(1)}, bf16[1152,640]{1,0:T(8,128)(2,1)}, u32[]{:S(2)}) copy-start(bf16[1152,640]{1,0:T(8,128)(2,1)} %constant.33.clone.table_ref.ready_ref) | copy-start | bytes 4423684
  1.5 6.1 %collective-permute-start = (f32[256,128]{1,0:T(8,128)S(1)}, f32[256,128]{1,0:T(8,128)S(1)}, u32[]{:S(2)}, u32[]{:S(2)}) collective-permute-start(f32[256,128]{1,0:T(8,128)S(1)} %pad_maximum_fusion), channel_id=1, source_target_pairs={{0,1},{1,2},{2,3},{4,5},{5,6},{6,7},{8,9},{9,10},{10,11},{12,13},{... | collective-permute-start | bytes 393224 | tf_op jit(solution)/shard_map/ppermute | solution.py:487
  5.0 6.9 %collective-permute-start.1 = (f32[256,128]{1,0:T(8,128)S(1)}, f32[256,128]{1,0:T(8,128)S(1)}, u32[]{:S(2)}, u32[]{:S(2)}) collective-permute-start(f32[256,128]{1,0:T(8,128)S(1)} %pad_maximum_fusion.1), channel_id=1, source_target_pairs={{1,0},{2,1},{3,2},{5,4},{6,5},{7,6},{9,8},{10,9},{11,10},{13,12},{... | collective-permute-start | bytes 393224 | tf_op jit(solution)/shard_map/ppermute | solution.py:486
  12.1 8.3 %collective-permute-start.2 = (f32[96,384]{1,0:T(8,128)S(1)}, f32[96,384]{1,0:T(8,128)S(1)}, u32[]{:S(2)}, u32[]{:S(2)}) collective-permute-start(f32[96,384]{1,0:T(8,128)S(1)} %get-tuple-element.21), channel_id=1, source_target_pairs={{0,4},{4,0},{8,12},{12,8},{16,20},{20,16},{24,28},{28,24},{1,5},{5... | collective-permute-start | bytes 442376 | tf_op jit(solution)/shard_map/ppermute | solution.py:495
  14.0 7.7 %collective-permute-start.3 = (f32[96,384]{1,0:T(8,128)S(1)}, f32[96,384]{1,0:T(8,128)S(1)}, u32[]{:S(2)}, u32[]{:S(2)}) collective-permute-start(f32[96,384]{1,0:T(8,128)S(1)} %get-tuple-element.22), channel_id=1, source_target_pairs={{4,8},{8,4},{12,16},{16,12},{20,24},{24,20},{5,9},{9,5},{13,17},{1... | collective-permute-start | bytes 442376 | tf_op jit(solution)/shard_map/ppermute | solution.py:495
  18.9 2.8 %copy-start.6 = (bf16[512,512]{1,0:T(8,128)(2,1)S(1)}, bf16[512,512]{1,0:T(8,128)(2,1)}, u32[]{:S(2)}) copy-start(bf16[512,512]{1,0:T(8,128)(2,1)} %constant.37.clone.col_out_ref) | copy-start | bytes 1572868
  18.9 2.8 %copy-start.7 = (bf16[384,576]{1,0:T(8,128)(2,1)S(1)}, bf16[384,576]{1,0:T(8,128)(2,1)}, u32[]{:S(2)}) copy-start(bf16[384,576]{1,0:T(8,128)(2,1)} %constant.35.clone.row_in_ref) | copy-start | bytes 1327108
  18.9 2.8 %copy-start.8 = (bf16[320,576]{1,0:T(8,128)(2,1)S(1)}, bf16[320,576]{1,0:T(8,128)(2,1)}, u32[]{:S(2)}) copy-start(bf16[320,576]{1,0:T(8,128)(2,1)} %constant.36.clone.row_out_ref) | copy-start | bytes 1105924
  18.9 2.8 %copy-start.9 = (bf16[384,192]{1,0:T(8,128)(2,1)S(1)}, bf16[384,192]{1,0:T(8,128)(2,1)}, u32[]{:S(2)}) copy-start(bf16[384,192]{1,0:T(8,128)(2,1)} %constant.34.clone.row_margin_ref) | copy-start | bytes 442372
  46.3 11.8 %collective-permute-start.4 = (f32[32,256]{1,0:T(8,128)S(1)}, f32[32,256]{1,0:T(8,128)S(1)}, u32[]{:S(2)}, u32[]{:S(2)}) collective-permute-start(f32[32,256]{1,0:T(8,128)S(1)} %reduce_sum.9), channel_id=1, source_target_pairs={{0,32},{32,0},{1,33},{33,1},{2,34},{34,2},{3,35},{35,3},{4,36},{36... | collective-permute-start | bytes 98312 | tf_op jit(solution)/shard_map/ppermute | solution.py:503
